TPU v7x, 32 devices: a whole 2x2x4 slice. The times are simulated.
32 devices in a mesh: groups: 2 (over x), ep: 16 (over z, y, core).
Axes of the slice: x: 2, y: 2, z: 4, core: 2. Of those that a mesh axis runs over, the one named last changes fastest.
Arguments:
- tokens: bfloat16 [1024, 3584], P(('groups', 'ep')), parts along dimension 0, may hold values from -6 to 6
- routes: int32 [1024, 8], P(('groups', 'ep')), parts along dimension 0, may hold values from 0 to 255, all different within a row; in each aligned block of 32 rows (0 to 31, 32 to 63, ...) at most 2 rows name the same one
- gate_num: int32 [1024, 8], P(('groups', 'ep')), parts along dimension 0, may hold values from 1 to 255
- w_gate: bfloat16 [16, 3584, 512], P('ep'), may hold values from -0.09375 to 0.09375
- w_up: bfloat16 [16, 3584, 512], P('ep'), may hold values from -0.09375 to 0.09375
- w_down: bfloat16 [16, 512, 3584], P('ep'), may hold values from -0.1875 to 0.1875
Outputs:
- combined: bfloat16 [1024, 3584], P(('groups', 'ep')), parts along dimension 0
There are 2 independent parts, one for each index of `groups`. A program takes and returns all parts, laid end to end along the dimension named above; an argument that names none is the same for every part. Nothing has to cross between parts.
Inputs may be any that keep to these rules, and one draw needn't show every extreme that they name: `routes`: each row names 8 different experts; among the 32 rows of one device no expert is named more than 2 times, a bound that some block reaches.
All inputs are finite; a program needn't handle non-finite values.
Results may differ from a plain program's by a relative error of at most 0.0058.
Values may be sent and summed in bfloat16 or wider, within the bound.
No kernel may reach another device: no remote copies, remote signals or barrier semaphores. Data moves between devices by JAX's collectives and lax.ppermute only.
A program may use at most 64 MiB of HBM per device.

v0:
```python
import jax
import jax.numpy as jnp
from jax import lax
from jax.sharding import PartitionSpec as P

SPLIT = 2
EXPERTS = 256


def partner_2(block, axis, apart):
    count = lax.axis_size(axis)
    route = []
    for low in range(count):
        high = low | 1 << apart
        if high != low and high < count:
            route += [(low, high), (high, low)]
    return lax.ppermute(block, axis, route)


def expert_mlp(received, w_gate, w_up, w_down):
    local_count = w_gate.shape[0]
    senders = received.shape[0] // local_count
    slot_count = received.shape[1]
    feature_width = received.shape[2]
    blocks = received.reshape(senders, local_count, slot_count, feature_width)
    gate_part = jnp.einsum("secd,edf->secf", blocks, w_gate, preferred_element_type=jnp.float32)
    up_part = jnp.einsum("secd,edf->secf", blocks, w_up, preferred_element_type=jnp.float32)
    hidden = (jax.nn.silu(gate_part) * up_part).astype(jnp.bfloat16)
    output = jnp.einsum("secf,efd->secd", hidden, w_down, preferred_element_type=jnp.float32)
    return output.reshape(senders * local_count, slot_count, feature_width)


def serve_rows(received, w_gate, w_up, w_down):
    parity = lax.axis_index("ep") % 2
    partner = partner_2(received, "ep", 0)
    lower_rows = jnp.where(parity == 0, received, partner)
    upper_rows = jnp.where(parity == 0, partner, received)
    whole_rows = jnp.concatenate([lower_rows, upper_rows], axis=2)
    results = expert_mlp(whole_rows, w_gate, w_up, w_down)
    half_width = results.shape[2] // 2
    lower_out = results[:, :, :half_width]
    upper_out = results[:, :, half_width:]
    kept = jnp.where(parity == 0, lower_out, upper_out)
    sending = jnp.where(parity == 0, upper_out, lower_out)
    arrived = partner_2(sending, "ep", 0)
    summed = (kept + arrived).astype(jnp.bfloat16)
    return lax.all_to_all(summed, "ep", split_axis=0, concat_axis=0, tiled=True)


def shards(tokens, routes, gate_num, w_gate, w_up, w_down):
    tok_rows, top_count = routes.shape
    feature_width = tokens.shape[1]
    devices_all = lax.axis_size("ep")
    experts_all = devices_all // SPLIT
    capacity = max(2, min(tok_rows, 5 * tok_rows * top_count // (2 * EXPERTS)))
    flat_routes = routes.reshape(-1)
    served = flat_routes < experts_all
    one_hot = (flat_routes[:, None] == jnp.arange(experts_all, dtype=jnp.int32)[None, :]).astype(
        jnp.int32
    )
    before = jnp.cumsum(one_hot, axis=0) - one_hot
    position = jnp.sum(before * one_hot, axis=1)
    slot_total = experts_all * capacity
    slot_index = jnp.where(served, flat_routes * capacity + position, slot_total)
    token_of = jnp.arange(tok_rows * top_count, dtype=jnp.int32) // top_count
    source_row = jnp.zeros((slot_total,), jnp.int32).at[slot_index].set(token_of, mode="drop")
    filled = jnp.zeros((slot_total,), jnp.bool_).at[slot_index].set(True, mode="drop")
    outgoing = jnp.where(filled[:, None], tokens[source_row], jnp.zeros((), tokens.dtype))
    outgoing = outgoing.reshape(experts_all, capacity, feature_width)
    half_width = feature_width // SPLIT
    outgoing = outgoing.reshape(experts_all, capacity, SPLIT, half_width)
    outgoing = outgoing.transpose(0, 2, 1, 3).reshape(experts_all * SPLIT, capacity, half_width)
    received = lax.all_to_all(outgoing, "ep", split_axis=0, concat_axis=0, tiled=True)
    returned = serve_rows(received, w_gate, w_up, w_down)
    returned = returned.reshape(experts_all, SPLIT, capacity, half_width)
    expert_rows = returned.transpose(0, 2, 1, 3).reshape(experts_all, capacity, feature_width)
    safe_route = jnp.where(served, flat_routes, 0)
    picked = expert_rows[safe_route, position]
    picked = picked.reshape(tok_rows, top_count, feature_width)
    gate_real = jnp.where(
        served.reshape(tok_rows, top_count), gate_num.astype(jnp.float32) / 256.0, 0.0
    )
    weights = gate_real.astype(jnp.bfloat16)
    combined = jnp.einsum("tk,tkd->td", weights, picked, preferred_element_type=jnp.float32)
    return combined.astype(jnp.bfloat16)


def solution(mesh):
    return jax.shard_map(
        shards,
        mesh=mesh,
        in_specs=(
            P(("groups", "ep"), None),
            P(("groups", "ep"), None),
            P(("groups", "ep"), None),
            P("ep", None, None),
            P("ep", None, None),
            P("ep", None, None),
        ),
        out_specs=P(("groups", "ep"), None),
        check_vma=False,
    )
```

profile of v0, /device:TPU:0, one launch (start us, length us, event | category | flops | bytes accessed | tf_op | source)
XLA Modules:
  0.0 48.8 jit_solution(16190040157651471799)
XLA Ops:
  0.0 0.0 copy-start
  0.0 0.8 %copy.16 = s32[32,8]{1,0:T(8,128)S(1)} copy(s32[32,8]{0,1:T(8,128)} %param.7) | data formatting | bytes 2048 | tf_op args[1]
  0.8 0.1 eq.38
  0.9 0.1 eq.34
  1.0 0.1 reshape.134
  1.1 0.6 %reduce-window.6 = s32[8,2,128]{2,0,1:T(8,128)S(1)} reduce-window(s32[8,2,128]{2,0,1:T(8,128)S(1)} %fusion.22, s32[]{:T(128)} %constant.50.clone.1), window={size=1x1x128 pad=0_0x0_0x127_0}, to_apply=%region_0.0 | reduce-window | flops 260096 | bytes 16388 | tf_op jit(solution)/shard_map/reduce-window
  1.7 0.2 slice_reduce_fusion
  1.9 0.1 fusion.21
  2.0 1.4 %scatter_custom_fusion.1 = s32[16]{0:T(128)S(1)} fusion(s32[256]{0:T(256)S(1)} %bitcast.73, s32[256]{0:T(256)S(1)} %and_select_fusion, s32[]{:T(128)} %constant.50.clone.1), kind=kCustom, calls=%fused_computation.52 | custom fusion | bytes 68 | tf_op jit(solution)/shard_map/scatter | solution.py:66
  3.5 1.5 %scatter_custom_fusion = pred[16]{0:T(512)(128)(4,1)S(1)} fusion(s32[256]{0:T(256)S(1)} %bitcast.74, pred[256]{0:T(512)(128)(4,1)S(1)} %broadcast.151, pred[]{:T(512)} %constant.53.clone.1), kind=kCustom, calls=%fused_computation.50 | custom fusion | bytes 17 | tf_op jit(solution)/shard_map/scatter | solution.py:67
  5.0 0.1 broadcast_in_dim.38
  5.1 0.0 copy-done
  5.1 0.6 %gather_fusion = bf16[16,3584]{1,0:T(8,128)(2,1)S(1)} fusion(bf16[32,3584]{1,0:T(8,128)(2,1)S(1)} %copy-done, s32[1024]{0:T(1024)S(1)} %pad_clamp_fusion), kind=kCustom, calls=%fused_computation | custom fusion | bytes 229440 | tf_op jit(solution)/shard_map/gather | solution.py:68
  5.7 0.2 fusion.14
  5.9 0.1 copy.19
  6.0 14.9 %all_to_all.10 = bf16[16,2,1792]{2,1,0:T(2,128)(2,1)S(1)} all-to-all(bf16[16,2,1792]{2,1,0:T(2,128)(2,1)S(1)} %bitcast.70), channel_id=1, replica_groups=mesh['groups'=2,'ep'=16] {'ep'}, dimensions={0} | all-to-all | bytes 229376 | tf_op jit(solution)/shard_map/all_to_all | solution.py:73
  20.9 0.1 collective-permute-start
  21.0 1.3 %collective-permute-done = bf16[16,2,1792]{2,0,1:T(8,128)(2,1)S(1)} collective-permute-done((bf16[16,2,1792]{2,0,1:T(8,128)(2,1)S(1)}, bf16[16,2,1792]{2,0,1:T(8,128)(2,1)S(1)}, u32[]{:S(2)}, u32[]{:S(2)}) %collective-permute-start) | collective-permute-done | bytes 114720 | tf_op jit(solution)/shard_map/ppermute | solution.py:17
  22.3 2.8 %fusion.8 = f32[16,1,2,512]{3,0,2,1:T(8,128)S(1)} fusion(bf16[1,3584,512]{2,1,0:T(8,128)(2,1)} %param.9, bf16[16,2,1792]{2,0,1:T(8,128)(2,1)S(1)} %get-tuple-element.6, bf16[16,2,1792]{2,0,1:T(8,128)(2,1)S(1)} %get-tuple-element.5), kind=kOutput, calls=%fused_computation.12 | convolution fusion | flops 117899264 | bytes 3964928 | tf_op jit(solution)/shard_map/secd,edf->secf/dot_general | solution.py:26
  25.1 0.0 copy-start.1
  25.1 0.0 copy-start.2
  25.1 4.6 %fusion = f32[16,2,3584]{2,0,1:T(8,128)S(1)} fusion(bf16[1,512,3584]{2,1,0:T(8,128)(2,1)} %param.11, f32[16,1,2,512]{3,0,2,1:T(8,128)S(1)} %fusion.8, bf16[1,3584,512]{2,1,0:T(8,128)(2,1)} %param.10, bf16[16,2,1792]{2,0,1:T(8,128)(2,1)S(1)} %get-tuple-element.6, bf16[16,2,1792]{2,0,1:T(8,128)(2,1)S(1)} %get-tuple-element.5), kind=kOutput, calls=%fused_computation.4 | convolution fusion | flops 235438080 | bytes 8093696 | tf_op jit(solution)/shard_map/secf,efd->secd/dot_general | solution.py:29
  29.7 0.2 collective-permute-start.1
  29.9 1.3 %collective-permute-done.1 = f32[16,2,1792]{2,0,1:T(8,128)S(1)} collective-permute-done((f32[16,2,1792]{2,0,1:T(8,128)S(1)}, f32[16,2,1792]{2,0,1:T(8,128)S(1)}, u32[]{:S(2)}, u32[]{:S(2)}) %collective-permute-start.1) | collective-permute-done | bytes 229408 | tf_op jit(solution)/shard_map/ppermute | solution.py:17
  31.3 0.7 %copy.23 = bf16[16,2,1792]{2,1,0:T(2,128)(2,1)} copy(bf16[16,2,1792]{2,0,1:T(8,128)(2,1)S(1)} %add_convert_fusion) | data formatting | bytes 229376 | tf_op jit(solution)/shard_map/convert_element_type | solution.py:46
  32.0 3.5 %all-to-all-start.1 = ((bf16[16,2,1792]{2,1,0:T(2,128)(2,1)}), bf16[16,2,1792]{2,1,0:T(2,128)(2,1)S(1)}, u32[]{:S(2)}, u32[]{:S(2)}) async-start(bf16[16,2,1792]{2,1,0:T(2,128)(2,1)} %copy.23), calls=%async_computation.1 | async-start | bytes 229376 | tf_op jit(solution)/shard_map/all_to_all | solution.py:47
  35.6 0.0 copy-done.1
  35.6 0.0 copy-done.2
  35.6 0.1 copy.25
  35.7 7.5 %all-to-all-done.1 = bf16[16,2,1792]{2,1,0:T(2,128)(2,1)S(1)} async-done(((bf16[16,2,1792]{2,1,0:T(2,128)(2,1)}), bf16[16,2,1792]{2,1,0:T(2,128)(2,1)S(1)}, u32[]{:S(2)}, u32[]{:S(2)}) %all-to-all-start.1) | async-done | bytes 114720 | tf_op jit(solution)/shard_map/all_to_all | solution.py:47
  43.2 0.1 copy.32
  43.3 0.1 reshape.142
  43.3 4.1 %gather_fusion.1 = bf16[256,3584]{1,0:T(8,128)(2,1)S(1)} fusion(bf16[8,2,3584]{2,1,0:T(2,128)(2,1)S(1)} %reshape.142, s32[256]{0:T(256)S(1)} %bitcast.68), kind=kCustom, calls=%fused_computation.1 | custom fusion | bytes 3672064 | tf_op jit(solution)/shard_map/gather | solution.py:78
  47.5 0.6 %fusion.6 = bf16[32,1,3584]{2,1,0:T(2,128)(2,1)S(1)} fusion(bf16[32,8,1]{1,2,0:T(2,128)(2,1)S(1)} %copy.25, bf16[256,3584]{1,0:T(8,128)(2,1)S(1)} %gather_fusion.1), kind=kOutput, calls=%fused_computation.10 | convolution fusion | flops 1835008 | bytes 2064896 | tf_op jit(solution)/shard_map/tk,tkd->td/dot_general | solution.py:84
  48.1 0.7 %copy.31 = bf16[32,1,3584]{2,0,1:T(8,128)(2,1)} copy(bf16[32,1,3584]{2,1,0:T(2,128)(2,1)S(1)} %fusion.6) | data formatting | bytes 458752 | tf_op jit(solution)/shard_map/tk,tkd->td/dot_general | solution.py:84
  (14 shorter events, 0.2 us)
Async XLA Ops:
  0.0 5.1 %copy-start = (bf16[32,3584]{1,0:T(8,128)(2,1)S(1)}, bf16[32,3584]{1,0:T(8,128)(2,1)}, u32[]{:S(2)}) copy-start(bf16[32,3584]{1,0:T(8,128)(2,1)} %param.6) | copy-start | bytes 688132
  20.9 1.4 %collective-permute-start = (bf16[16,2,1792]{2,0,1:T(8,128)(2,1)S(1)}, bf16[16,2,1792]{2,0,1:T(8,128)(2,1)S(1)}, u32[]{:S(2)}, u32[]{:S(2)}) collective-permute-start(bf16[16,2,1792]{2,0,1:T(8,128)(2,1)S(1)} %copy.21), channel_id=1, source_target_pairs={{0,1},{1,0},{2,3},{3,2},{4,5},{5,4},{6,7},{7,6},{8,9},{9,8},{10,11... | collective-permute-start | bytes 344072 | tf_op jit(solution)/shard_map/ppermute | solution.py:17
  25.1 10.5 %copy-start.1 = (s32[32,8]{0,1:T(8,128)S(1)}, s32[32,8]{0,1:T(8,128)}, u32[]{:S(2)}) copy-start(s32[32,8]{0,1:T(8,128)} %param.7) | copy-start | bytes 3076
  25.1 10.5 %copy-start.2 = (s32[32,8]{0,1:T(8,128)S(1)}, s32[32,8]{0,1:T(8,128)}, u32[]{:S(2)}) copy-start(s32[32,8]{0,1:T(8,128)} %param.8) | copy-start | bytes 3076
  29.7 1.6 %collective-permute-start.1 = (f32[16,2,1792]{2,0,1:T(8,128)S(1)}, f32[16,2,1792]{2,0,1:T(8,128)S(1)}, u32[]{:S(2)}, u32[]{:S(2)}) collective-permute-start(f32[16,2,1792]{2,0,1:T(8,128)S(1)} %slice_select_fusion), channel_id=1, source_target_pairs={{0,1},{1,0},{2,3},{3,2},{4,5},{5,4},{6,7},{7,6},{8,9},{9,8},{10,11... | collective-permute-start | bytes 688136 | tf_op jit(solution)/shard_map/ppermute | solution.py:17
  32.0 11.1 %all-to-all-start.1 = ((bf16[16,2,1792]{2,1,0:T(2,128)(2,1)}), bf16[16,2,1792]{2,1,0:T(2,128)(2,1)S(1)}, u32[]{:S(2)}, u32[]{:S(2)}) async-start(bf16[16,2,1792]{2,1,0:T(2,128)(2,1)} %copy.23), calls=%async_computation.1 | async-start | bytes 229376 | tf_op jit(solution)/shard_map/all_to_all | solution.py:47
where the time goes:
time: 49.1 us; the launch traced here: 48.8 us
  blocking collectives  14.9 us (30%)
  local copies, waits for them, and re-layouts  10.9 us (22%)
  waiting for transfers between devices  10.1 us (21%)
  matrix products  7.98 us (16%)
  starting transfers between devices  3.8 us (8%)
  other arithmetic  1.01 us (2%)
    all_to_all x1, blocking collectives, shards(): lax.all_to_all(outgoing, 'ep', split_axis=0, concat_axis=0, tiled=True)  14.9 us
    all_to_all x1, waiting for transfers between devices, serve_rows(): return lax.all_to_all(summed, 'ep', split_axis=0, concat_axis=0, tiled=True)  7.48 us
    dot_general x1, matrix products, expert_mlp(): jnp.einsum('secf,efd->secd', hidden, w_down, preferred_element_type=jnp.f...  4.61 us
    gather x1, local copies, waits for them, and re-layouts, shards(): picked = expert_rows[safe_route, position]  4.12 us
    all_to_all x1, starting transfers between devices, serve_rows(): return lax.all_to_all(summed, 'ep', split_axis=0, concat_axis=0, tiled=True)  3.51 us
    dot_general x1, matrix products, expert_mlp(): jnp.einsum('secd,edf->secf', blocks, w_gate, preferred_element_type=jnp.f...  2.76 us
    ppermute x2, waiting for transfers between devices, partner_2(): return lax.ppermute(block, axis, route)  2.64 us
    scatter x1, local copies, waits for them, and re-layouts, shards(): jnp.zeros((slot_total,), jnp.bool_).at[slot_index].set(True, mode='drop')  1.49 us
  transfers between devices with their start and end apart: 3, of which 3 were waited for; matrix products, arithmetic and copies ran while one was open for 0% of the time, Pallas kernels for 0%

commit v1 on v0

v1 whole, which is shorter than its diff:
```python
import functools
import jax
import jax.numpy as jnp
from jax import lax
from jax.experimental import pallas as pl
from jax.experimental.pallas import tpu as pltpu
from jax.sharding import PartitionSpec as P

SPLIT = 2
EXPERTS = 256


def choose(routes, gates, slots, capacity):
    rows, top = routes.shape
    slot = lax.broadcasted_iota(jnp.int32, (rows, slots), 1)
    expert, place = slot // capacity, slot % capacity
    hit = jnp.zeros((rows, slots), jnp.float32)
    gate = jnp.zeros((rows, slots), jnp.float32)
    for k in range(top):
        same = routes[:, k : k + 1] == expert
        hit = jnp.where(same, 1.0, hit)
        gate = jnp.where(same, gates[:, k : k + 1].astype(jnp.float32) / 256.0, gate)
    earlier = lax.broadcasted_iota(jnp.int32, (rows, rows), 0) > lax.broadcasted_iota(
        jnp.int32, (rows, rows), 1
    )
    rank = jnp.dot(
        earlier.astype(jnp.bfloat16), hit.astype(jnp.bfloat16), preferred_element_type=jnp.float32
    )
    mine = rank == place.astype(jnp.float32)
    return jnp.where(mine, hit, 0.0).astype(jnp.bfloat16), jnp.where(mine, gate, 0.0).astype(
        jnp.bfloat16
    )


def route_kernel(capacity, routes_ref, gates_ref, tokens_ref, out_ref, weight_ref):
    chips = out_ref.shape[0]
    pick, weight = choose(routes_ref[...], gates_ref[...], chips * capacity, capacity)
    weight_ref[...] = weight
    rows = lax.dot_general(
        pick, tokens_ref[...], (((0,), (0,)), ((), ())), preferred_element_type=jnp.float32
    ).astype(jnp.bfloat16)
    out_ref[...] = rows.reshape(out_ref.shape)


def mlp_kernel(own_ref, other_ref, gate_ref, up_ref, down_ref, keep_ref, send_ref):
    shape = own_ref.shape
    flat = (shape[0] * shape[1], shape[2])
    x = jnp.concatenate([own_ref[...].reshape(flat), other_ref[...].reshape(flat)], axis=0)
    gate = jnp.dot(x, gate_ref[0], preferred_element_type=jnp.float32)
    up = jnp.dot(x, up_ref[0], preferred_element_type=jnp.float32)
    hidden = (gate / (1.0 + jnp.exp(-gate)) * up).astype(jnp.bfloat16)
    out = jnp.dot(hidden, down_ref[0], preferred_element_type=jnp.float32)
    keep_ref[...] = out[: flat[0]].reshape(shape)
    send_ref[...] = out[flat[0] :].astype(jnp.bfloat16).reshape(shape)


def combine_kernel(weight_ref, rows_ref, out_ref):
    shape = rows_ref.shape
    rows = rows_ref[...].reshape(shape[0] * shape[1], shape[2])
    out_ref[...] = jnp.dot(weight_ref[...], rows, preferred_element_type=jnp.float32).astype(
        jnp.bfloat16
    )


VMEM = pl.BlockSpec(memory_space=pltpu.VMEM)
LIMIT = pltpu.CompilerParams(vmem_limit_bytes=16 << 20)


def shards(tokens, routes, gate_num, w_gate, w_up, w_down):
    tok_rows, top_count = routes.shape
    width = tokens.shape[1]
    devices = lax.axis_size("ep")
    chips = devices // SPLIT
    capacity = max(2, min(tok_rows, 5 * tok_rows * top_count // (2 * EXPERTS)))
    same_core = [[c * SPLIT + k for c in range(chips)] for k in range(SPLIT)]
    swap = [(d, d ^ 1) for d in range(devices)]
    block = (chips, capacity, width)
    outgoing, weight = pl.pallas_call(
        functools.partial(route_kernel, capacity),
        out_shape=(
            jax.ShapeDtypeStruct(block, jnp.bfloat16),
            jax.ShapeDtypeStruct((tok_rows, chips * capacity), jnp.bfloat16),
        ),
        in_specs=[VMEM] * 3,
        out_specs=(VMEM, VMEM),
        name="route",
        cost_estimate=pl.CostEstimate(flops=10**10, bytes_accessed=10**8, transcendentals=0),
        compiler_params=LIMIT,
    )(routes, gate_num, tokens)
    own = lax.all_to_all(
        outgoing, "ep", split_axis=0, concat_axis=0, tiled=True, axis_index_groups=same_core
    )
    other = lax.ppermute(own, "ep", swap)
    weights = [pltpu.with_memory_space_constraint(w, pltpu.VMEM) for w in (w_gate, w_up, w_down)]
    keep, send = pl.pallas_call(
        mlp_kernel,
        out_shape=(
            jax.ShapeDtypeStruct(block, jnp.float32),
            jax.ShapeDtypeStruct(block, jnp.bfloat16),
        ),
        in_specs=[VMEM] * 5,
        out_specs=(VMEM, VMEM),
        name="mlp",
        compiler_params=LIMIT,
    )(own, other, *weights)
    arrived = lax.ppermute(send, "ep", swap)
    summed = (keep + arrived.astype(jnp.float32)).astype(jnp.bfloat16)
    returned = lax.all_to_all(
        summed, "ep", split_axis=0, concat_axis=0, tiled=True, axis_index_groups=same_core
    )
    return pl.pallas_call(
        combine_kernel,
        out_shape=jax.ShapeDtypeStruct((tok_rows, width), jnp.bfloat16),
        in_specs=[VMEM] * 2,
        out_specs=VMEM,
        name="combine",
        compiler_params=LIMIT,
    )(weight, returned)


def solution(mesh):
    return jax.shard_map(
        shards,
        mesh=mesh,
        in_specs=(
            P(("groups", "ep"), None),
            P(("groups", "ep"), None),
            P(("groups", "ep"), None),
            P("ep", None, None),
            P("ep", None, None),
            P("ep", None, None),
        ),
        out_specs=P(("groups", "ep"), None),
        check_vma=False,
    )
```

time: 49.1 us -> 33.3 us (0.68)
  blocking collectives: 14.9 us -> 24.3 us
  local copies, waits for them, and re-layouts: 10.9 us -> 2.47 us
  matrix products: 7.98 us -> 0 us
  waiting for transfers between devices: 10.1 us -> 2.5 us
  starting transfers between devices: 3.8 us -> 0.22 us
  Pallas kernels: 0 us -> 3.39 us
  other arithmetic: 1.01 us -> 0.13 us
    all_to_all x1 -> x2, blocking collectives: 14.9 us -> 24.3 us  [the longest x1 14.6 us: shards(): lax.all_to_all(outgoing, 'ep', split_axis=0, concat_axis=0, tiled=True, a...]
    dot_general x3 -> x0, matrix products: 7.98 us -> none  [the longest x1 4.61 us: expert_mlp(): jnp.einsum('secf,efd->secd', hidden, w_down, preferred_element_type=jnp.f...]
    all_to_all x1 -> x0, waiting for transfers between devices: 7.48 us -> none  [serve_rows(): return lax.all_to_all(summed, 'ep', split_axis=0, concat_axis=0, tiled=True)]
    gather x3 -> x0, local copies, waits for them, and re-layouts: 4.77 us -> none  [the longest x1 4.12 us: shards(): picked = expert_rows[safe_route, position]]
    all_to_all x1 -> x0, starting transfers between devices: 3.51 us -> none  [serve_rows(): return lax.all_to_all(summed, 'ep', split_axis=0, concat_axis=0, tiled=True)]
    pallas_call x0 -> x3, Pallas kernels: none -> 3.39 us  [the longest x1 2.06 us: shards(): pl.pallas_call(mlp_kernel, out_shape=(jax.ShapeDtypeStruct(block, jnp.flo...]
    scatter x2 -> x0, local copies, waits for them, and re-layouts: 2.88 us -> none  [the longest x1 1.49 us: shards(): jnp.zeros((slot_total,), jnp.bool_).at[slot_index].set(True, mode='drop')]
    unnamed x7 -> x10, local copies, waits for them, and re-layouts: 0.82 us -> 2.47 us
  transfers between devices with their start and end apart: 3 -> 2, of which waited for: 3 -> 2; matrix products, arithmetic and copies ran while one was open for 0% -> 0% of each run, Pallas kernels for 0% -> 0%
where the time goes in v1:
time: 33.3 us; the launch traced here: 33.1 us
  blocking collectives  24.3 us (73%)
  Pallas kernels  3.39 us (10%)
  waiting for transfers between devices  2.5 us (8%)
  local copies, waits for them, and re-layouts  2.47 us (7%)
    all_to_all x1, blocking collectives, shards(): lax.all_to_all(outgoing, 'ep', split_axis=0, concat_axis=0, tiled=True, a...  14.6 us
    all_to_all x1, blocking collectives, shards(): lax.all_to_all(summed, 'ep', split_axis=0, concat_axis=0, tiled=True, axi...  9.73 us
    unnamed x10, local copies, waits for them, and re-layouts  2.47 us
    pallas_call x1, Pallas kernels, shards(): pl.pallas_call(mlp_kernel, out_shape=(jax.ShapeDtypeStruct(block, jnp.flo...  2.06 us
    ppermute x1, waiting for transfers between devices, shards(): other = lax.ppermute(own, 'ep', swap)  1.32 us
    ppermute x1, waiting for transfers between devices, shards(): arrived = lax.ppermute(send, 'ep', swap)  1.18 us
    pallas_call x1, Pallas kernels, shards(): pl.pallas_call(combine_kernel, out_shape=jax.ShapeDtypeStruct((tok_rows,...  0.89 us
  transfers between devices with their start and end apart: 2, of which 2 were waited for; matrix products, arithmetic and copies ran while one was open for 0% of the time, Pallas kernels for 0%

profile of v1, /device:TPU:0, one launch (start us, length us, event | category | flops | bytes accessed | tf_op | source)
XLA Modules:
  0.0 33.1 jit_solution(7933646350406260101)
XLA Ops:
  0.0 0.8 %copy.7.routes_ref = s32[32,8]{1,0:T(8,128)S(1)} copy(s32[32,8]{0,1:T(8,128)} %param.7) | data formatting | bytes 2048 | tf_op args[1]
  0.8 0.8 %copy.8.gates_ref = s32[32,8]{1,0:T(8,128)S(1)} copy(s32[32,8]{0,1:T(8,128)} %param.8) | data formatting | bytes 2048 | tf_op args[2]
  1.5 0.0 copy-start.3
  1.5 0.9 %copy-done.3 = bf16[32,3584]{1,0:T(8,128)(2,1)S(1)} copy-done((bf16[32,3584]{1,0:T(8,128)(2,1)S(1)}, bf16[32,3584]{1,0:T(8,128)(2,1)}, u32[]{:S(2)}) %copy-start.3) | copy-done | bytes 229400
  2.5 0.0 copy-start
  2.5 0.0 copy-start.1
  2.5 0.0 copy-start.2
  2.5 0.4 %route.1 = (bf16[8,2,3584]{2,1,0:T(2,128)(2,1)S(1)}, bf16[32,16]{1,0:T(8,128)(2,1)S(1)}) custom-call(s32[32,8]{1,0:T(8,128)S(1)} %copy.7.routes_ref, s32[32,8]{1,0:T(8,128)S(1)} %copy.8.gates_ref, bf16[32,3584]{1,0:T(8,128)(2,1)S(1)} %copy-done.3), custom_call_target="tpu_custom_call" | custom-call | flops 10000000000 | bytes 100000000 | tf_op jit(solution)/shard_map/route/pallas_call | solution.py:78
  2.9 14.6 %all_to_all.10.own_ref = bf16[8,2,3584]{2,1,0:T(2,128)(2,1)S(1)} all-to-all(bf16[8,2,3584]{2,1,0:T(2,128)(2,1)S(1)} %get-tuple-element.10), channel_id=1, replica_groups={{0,2,4,6,8,10,12,14},{1,3,5,7,9,11,13,15},{16,18,20,22,24,26,28,30},{17..., dimensions={0} | all-to-all | bytes 229376 | tf_op jit(solution)/shard_map/all_to_all | solution.py:90
  17.5 0.0 collective-permute-start
  17.5 1.3 %collective-permute-done.other_ref = bf16[8,2,3584]{2,1,0:T(2,128)(2,1)S(1)} collective-permute-done((bf16[8,2,3584]{2,1,0:T(2,128)(2,1)S(1)}, bf16[8,2,3584]{2,1,0:T(2,128)(2,1)S(1)}, u32[]{:S(2)}, u32[]{:S(2)}) %collective-permute-start) | collective-permute-done | bytes 114720 | tf_op jit(solution)/shard_map/ppermute | solution.py:93
  18.9 0.0 copy-done
  18.9 0.0 copy-done.1
  18.9 0.0 copy-done.2
  18.9 2.1 %mlp.1 = (f32[8,2,3584]{2,1,0:T(2,128)S(1)}, bf16[8,2,3584]{2,1,0:T(2,128)(2,1)S(1)}) custom-call(bf16[8,2,3584]{2,1,0:T(2,128)(2,1)S(1)} %all_to_all.10.own_ref, bf16[8,2,3584]{2,1,0:T(2,128)(2,1)S(1)} %collective-permute-done.other_ref, bf16[1,3584,512]{2,1,0:T(8,128)(2,1)S(1)} %copy-done, bf16[1,3584,512]{2,1,0:T(8,128)(2,1)S(1)} %copy-done.1, ...), custom_call_target="tpu_custom_call" | custom-call | tf_op jit(solution)/shard_map/mlp/pallas_call | solution.py:95
  20.9 0.2 collective-permute-start.1
  21.1 1.2 %collective-permute-done.1 = bf16[8,2,3584]{2,1,0:T(2,128)(2,1)S(1)} collective-permute-done((bf16[8,2,3584]{2,1,0:T(2,128)(2,1)S(1)}, bf16[8,2,3584]{2,1,0:T(2,128)(2,1)S(1)}, u32[]{:S(2)}, u32[]{:S(2)}) %collective-permute-start.1) | collective-permute-done | bytes 114720 | tf_op jit(solution)/shard_map/ppermute | solution.py:106
  22.3 0.1 add_convert_fusion
  22.5 9.7 %all_to_all.11.rows_ref = bf16[8,2,3584]{2,1,0:T(2,128)(2,1)S(1)} all-to-all(bf16[8,2,3584]{2,1,0:T(2,128)(2,1)S(1)} %add_convert_fusion), channel_id=1, replica_groups={{0,2,4,6,8,10,12,14},{1,3,5,7,9,11,13,15},{16,18,20,22,24,26,28,30},{17..., dimensions={0} | all-to-all | bytes 229376 | tf_op jit(solution)/shard_map/all_to_all | solution.py:108
  32.2 0.9 %combine.1 = bf16[32,3584]{1,0:T(8,128)(2,1)} custom-call(bf16[32,16]{1,0:T(8,128)(2,1)S(1)} %get-tuple-element.9.weight_ref, bf16[8,2,3584]{2,1,0:T(2,128)(2,1)S(1)} %all_to_all.11.rows_ref), custom_call_target="tpu_custom_call" | custom-call | tf_op jit(solution)/shard_map/combine/pallas_call | solution.py:111
Async XLA Ops:
  1.5 0.9 %copy-start.3 = (bf16[32,3584]{1,0:T(8,128)(2,1)S(1)}, bf16[32,3584]{1,0:T(8,128)(2,1)}, u32[]{:S(2)}) copy-start(bf16[32,3584]{1,0:T(8,128)(2,1)} %tokens_ref.1) | copy-start | bytes 688132
  2.5 16.4 %copy-start = (bf16[1,3584,512]{2,1,0:T(8,128)(2,1)S(1)}, bf16[1,3584,512]{2,1,0:T(8,128)(2,1)}, u32[]{:S(2)}) copy-start(bf16[1,3584,512]{2,1,0:T(8,128)(2,1)} %gate_ref.1) | copy-start | bytes 11010052
  2.5 16.4 %copy-start.1 = (bf16[1,3584,512]{2,1,0:T(8,128)(2,1)S(1)}, bf16[1,3584,512]{2,1,0:T(8,128)(2,1)}, u32[]{:S(2)}) copy-start(bf16[1,3584,512]{2,1,0:T(8,128)(2,1)} %up_ref.1) | copy-start | bytes 11010052
  2.5 16.4 %copy-start.2 = (bf16[1,512,3584]{2,1,0:T(8,128)(2,1)S(1)}, bf16[1,512,3584]{2,1,0:T(8,128)(2,1)}, u32[]{:S(2)}) copy-start(bf16[1,512,3584]{2,1,0:T(8,128)(2,1)} %down_ref.1) | copy-start | bytes 11010052
  17.5 1.3 %collective-permute-start = (bf16[8,2,3584]{2,1,0:T(2,128)(2,1)S(1)}, bf16[8,2,3584]{2,1,0:T(2,128)(2,1)S(1)}, u32[]{:S(2)}, u32[]{:S(2)}) collective-permute-start(bf16[8,2,3584]{2,1,0:T(2,128)(2,1)S(1)} %all_to_all.10.own_ref), channel_id=1, source_target_pairs={{0,1},{1,0},{2,3},{3,2},{4,5},{5,4},{6,7},{7,6},{8,9},{9,8},{10,11... | collective-permute-start | bytes 344072 | tf_op jit(solution)/shard_map/ppermute | solution.py:93
  20.9 1.4 %collective-permute-start.1 = (bf16[8,2,3584]{2,1,0:T(2,128)(2,1)S(1)}, bf16[8,2,3584]{2,1,0:T(2,128)(2,1)S(1)}, u32[]{:S(2)}, u32[]{:S(2)}) collective-permute-start(bf16[8,2,3584]{2,1,0:T(2,128)(2,1)S(1)} %get-tuple-element.12), channel_id=1, source_target_pairs={{0,1},{1,0},{2,3},{3,2},{4,5},{5,4},{6,7},{7,6},{8,9},{9,8},{10,11... | collective-permute-start | bytes 344072 | tf_op jit(solution)/shard_map/ppermute | solution.py:106

commit v2 on v1

--- a/solution.py
+++ b/solution.py
@@ -10,36 +10,36 @@
 EXPERTS = 256
 
 
-def choose(routes, gates, slots, capacity):
-    rows, top = routes.shape
-    slot = lax.broadcasted_iota(jnp.int32, (rows, slots), 1)
-    expert, place = slot // capacity, slot % capacity
-    hit = jnp.zeros((rows, slots), jnp.float32)
-    gate = jnp.zeros((rows, slots), jnp.float32)
-    for k in range(top):
-        same = routes[:, k : k + 1] == expert
-        hit = jnp.where(same, 1.0, hit)
-        gate = jnp.where(same, gates[:, k : k + 1].astype(jnp.float32) / 256.0, gate)
-    earlier = lax.broadcasted_iota(jnp.int32, (rows, rows), 0) > lax.broadcasted_iota(
+def slots_of(routes, slots, capacity, order):
+    top, rows = routes.shape
+    slot = lax.broadcasted_iota(jnp.int32, (slots, rows), 0)
+    block, place = slot // capacity, slot % capacity
+    expert = jnp.zeros_like(block)
+    for j, chip in enumerate(order):
+        expert = jnp.where(block == j, chip, expert)
+    same = [routes[k : k + 1, :] == expert for k in range(top)]
+    hit = functools.reduce(jnp.logical_or, same).astype(jnp.float32)
+    earlier = lax.broadcasted_iota(jnp.int32, (rows, rows), 0) < lax.broadcasted_iota(
         jnp.int32, (rows, rows), 1
     )
     rank = jnp.dot(
-        earlier.astype(jnp.bfloat16), hit.astype(jnp.bfloat16), preferred_element_type=jnp.float32
+        hit.astype(jnp.bfloat16), earlier.astype(jnp.bfloat16), preferred_element_type=jnp.float32
     )
-    mine = rank == place.astype(jnp.float32)
-    return jnp.where(mine, hit, 0.0).astype(jnp.bfloat16), jnp.where(mine, gate, 0.0).astype(
-        jnp.bfloat16
-    )
+    return jnp.where(rank == place.astype(jnp.float32), hit, 0.0), same
 
 
-def route_kernel(capacity, routes_ref, gates_ref, tokens_ref, out_ref, weight_ref):
+def route_kernel(capacity, order, routes_ref, gates_ref, tokens_ref, out_ref, weight_ref):
     chips = out_ref.shape[0]
-    pick, weight = choose(routes_ref[...], gates_ref[...], chips * capacity, capacity)
-    weight_ref[...] = weight
-    rows = lax.dot_general(
-        pick, tokens_ref[...], (((0,), (0,)), ((), ())), preferred_element_type=jnp.float32
+    pick, same = slots_of(routes_ref[...], chips * capacity, capacity, order)
+    rows = jnp.dot(
+        pick.astype(jnp.bfloat16), tokens_ref[...], preferred_element_type=jnp.float32
     ).astype(jnp.bfloat16)
     out_ref[...] = rows.reshape(out_ref.shape)
+    gates = gates_ref[...].astype(jnp.float32) / 256.0
+    weight = jnp.zeros_like(pick)
+    for k, chosen in enumerate(same):
+        weight = jnp.where(chosen, gates[k : k + 1, :], weight)
+    weight_ref[...] = (weight * pick).astype(jnp.bfloat16)
 
 
 def mlp_kernel(own_ref, other_ref, gate_ref, up_ref, down_ref, keep_ref, send_ref):
@@ -57,12 +57,18 @@
 def combine_kernel(weight_ref, rows_ref, out_ref):
     shape = rows_ref.shape
     rows = rows_ref[...].reshape(shape[0] * shape[1], shape[2])
-    out_ref[...] = jnp.dot(weight_ref[...], rows, preferred_element_type=jnp.float32).astype(
-        jnp.bfloat16
-    )
+    out_ref[...] = lax.dot_general(
+        weight_ref[...], rows, (((0,), (0,)), ((), ())), preferred_element_type=jnp.float32
+    ).astype(jnp.bfloat16)
+
+
+def group_order(chips):
+    first = (5 * chips) // 8
+    return [first] + [c for c in range(chips) if c != first]
 
 
 VMEM = pl.BlockSpec(memory_space=pltpu.VMEM)
+WHOLE = pl.BlockSpec()
 LIMIT = pltpu.CompilerParams(vmem_limit_bytes=16 << 20)
 
 
@@ -72,21 +78,22 @@
     devices = lax.axis_size("ep")
     chips = devices // SPLIT
     capacity = max(2, min(tok_rows, 5 * tok_rows * top_count // (2 * EXPERTS)))
-    same_core = [[c * SPLIT + k for c in range(chips)] for k in range(SPLIT)]
+    order = group_order(chips)
+    same_core = [[c * SPLIT + k for c in order] for k in range(SPLIT)]
     swap = [(d, d ^ 1) for d in range(devices)]
     block = (chips, capacity, width)
     outgoing, weight = pl.pallas_call(
-        functools.partial(route_kernel, capacity),
+        functools.partial(route_kernel, capacity, order),
         out_shape=(
             jax.ShapeDtypeStruct(block, jnp.bfloat16),
-            jax.ShapeDtypeStruct((tok_rows, chips * capacity), jnp.bfloat16),
+            jax.ShapeDtypeStruct((chips * capacity, tok_rows), jnp.bfloat16),
         ),
-        in_specs=[VMEM] * 3,
+        in_specs=[WHOLE] * 3,
         out_specs=(VMEM, VMEM),
         name="route",
         cost_estimate=pl.CostEstimate(flops=10**10, bytes_accessed=10**8, transcendentals=0),
         compiler_params=LIMIT,
-    )(routes, gate_num, tokens)
+    )(*(pltpu.with_memory_space_constraint(a, pltpu.HBM) for a in (routes.T, gate_num.T, tokens)))
     own = lax.all_to_all(
         outgoing, "ep", split_axis=0, concat_axis=0, tiled=True, axis_index_groups=same_core
     )

time: 33.3 us -> 28.2 us (0.85)
  blocking collectives: 24.3 us -> 20.8 us
  local copies, waits for them, and re-layouts: 2.47 us -> 0.01 us
  Pallas kernels: 3.39 us -> 4.39 us
    all_to_all x1, blocking collectives: 14.6 us -> 11.6 us  [shards(): lax.all_to_all(outgoing, 'ep', split_axis=0, concat_axis=0, tiled=True, a...]
    unnamed x10 -> x6, local copies, waits for them, and re-layouts: 2.47 us -> 0.01 us
    pallas_call x1, Pallas kernels: 0.44 us -> 1.41 us  [shards(): pl.pallas_call(functools.partial(route_kernel, capacity, order), out_shap...]
    all_to_all x1, blocking collectives: 9.73 us -> 9.15 us  [shards(): lax.all_to_all(summed, 'ep', split_axis=0, concat_axis=0, tiled=True, axi...]
where the time goes in v2:
time: 28.2 us; the launch traced here: 28 us
  blocking collectives  20.8 us (74%)
  Pallas kernels  4.39 us (16%)
  waiting for transfers between devices  2.5 us (9%)
    all_to_all x1, blocking collectives, shards(): lax.all_to_all(outgoing, 'ep', split_axis=0, concat_axis=0, tiled=True, a...  11.6 us
    all_to_all x1, blocking collectives, shards(): lax.all_to_all(summed, 'ep', split_axis=0, concat_axis=0, tiled=True, axi...  9.15 us
    pallas_call x1, Pallas kernels, shards(): pl.pallas_call(mlp_kernel, out_shape=(jax.ShapeDtypeStruct(block, jnp.flo...  2.07 us
    pallas_call x1, Pallas kernels, shards(): pl.pallas_call(functools.partial(route_kernel, capacity, order), out_shap...  1.41 us
    ppermute x1, waiting for transfers between devices, shards(): other = lax.ppermute(own, 'ep', swap)  1.32 us
    ppermute x1, waiting for transfers between devices, shards(): arrived = lax.ppermute(send, 'ep', swap)  1.18 us
    pallas_call x1, Pallas kernels, shards(): pl.pallas_call(combine_kernel, out_shape=jax.ShapeDtypeStruct((tok_rows,...  0.92 us
  transfers between devices with their start and end apart: 2, of which 2 were waited for; matrix products, arithmetic and copies ran while one was open for 0% of the time, Pallas kernels for 0%

profile of v2, /device:TPU:0, one launch (start us, length us, event | category | flops | bytes accessed | tf_op | source)
XLA Modules:
  0.0 28.0 jit_solution(397973621002553068)
XLA Ops:
  0.0 0.0 copy-start
  0.0 0.0 copy-start.1
  0.0 0.0 copy-start.2
  0.0 1.4 %route.1 = (bf16[8,2,3584]{2,1,0:T(2,128)(2,1)S(1)}, bf16[16,32]{1,0:T(8,128)(2,1)S(1)}) custom-call(s32[8,32]{1,0:T(8,128)} %bitcast.2, s32[8,32]{1,0:T(8,128)} %bitcast.3, bf16[32,3584]{1,0:T(8,128)(2,1)} %tokens_ref.1), custom_call_target="tpu_custom_call" | custom-call | flops 10000000000 | bytes 100000000 | tf_op jit(solution)/shard_map/route/pallas_call | solution.py:85
  1.4 11.6 %all_to_all.10.own_ref = bf16[8,2,3584]{2,1,0:T(2,128)(2,1)S(1)} all-to-all(bf16[8,2,3584]{2,1,0:T(2,128)(2,1)S(1)} %get-tuple-element.10), channel_id=1, replica_groups={{10,0,2,4,6,8,12,14},{11,1,3,5,7,9,13,15},{26,16,18,20,22,24,28,30},{27..., dimensions={0} | all-to-all | bytes 229376 | tf_op jit(solution)/shard_map/all_to_all | solution.py:97
  13.0 0.0 collective-permute-start
  13.0 1.3 %collective-permute-done.other_ref = bf16[8,2,3584]{2,1,0:T(2,128)(2,1)S(1)} collective-permute-done((bf16[8,2,3584]{2,1,0:T(2,128)(2,1)S(1)}, bf16[8,2,3584]{2,1,0:T(2,128)(2,1)S(1)}, u32[]{:S(2)}, u32[]{:S(2)}) %collective-permute-start) | collective-permute-done | bytes 114720 | tf_op jit(solution)/shard_map/ppermute | solution.py:100
  14.4 0.0 copy-done
  14.4 0.0 copy-done.1
  14.4 0.0 copy-done.2
  14.4 2.1 %mlp.1 = (f32[8,2,3584]{2,1,0:T(2,128)S(1)}, bf16[8,2,3584]{2,1,0:T(2,128)(2,1)S(1)}) custom-call(bf16[8,2,3584]{2,1,0:T(2,128)(2,1)S(1)} %all_to_all.10.own_ref, bf16[8,2,3584]{2,1,0:T(2,128)(2,1)S(1)} %collective-permute-done.other_ref, bf16[1,3584,512]{2,1,0:T(8,128)(2,1)S(1)} %copy-done, bf16[1,3584,512]{2,1,0:T(8,128)(2,1)S(1)} %copy-done.1, ...), custom_call_target="tpu_custom_call" | custom-call | tf_op jit(solution)/shard_map/mlp/pallas_call | solution.py:102
  16.4 0.2 collective-permute-start.1
  16.6 1.2 %collective-permute-done.1 = bf16[8,2,3584]{2,1,0:T(2,128)(2,1)S(1)} collective-permute-done((bf16[8,2,3584]{2,1,0:T(2,128)(2,1)S(1)}, bf16[8,2,3584]{2,1,0:T(2,128)(2,1)S(1)}, u32[]{:S(2)}, u32[]{:S(2)}) %collective-permute-start.1) | collective-permute-done | bytes 114720 | tf_op jit(solution)/shard_map/ppermute | solution.py:113
  17.8 0.1 add_convert_fusion
  18.0 9.2 %all_to_all.11.rows_ref = bf16[8,2,3584]{2,1,0:T(2,128)(2,1)S(1)} all-to-all(bf16[8,2,3584]{2,1,0:T(2,128)(2,1)S(1)} %add_convert_fusion), channel_id=1, replica_groups={{10,0,2,4,6,8,12,14},{11,1,3,5,7,9,13,15},{26,16,18,20,22,24,28,30},{27..., dimensions={0} | all-to-all | bytes 229376 | tf_op jit(solution)/shard_map/all_to_all | solution.py:115
  27.1 0.9 %combine.1 = bf16[32,3584]{1,0:T(8,128)(2,1)} custom-call(bf16[16,32]{1,0:T(8,128)(2,1)S(1)} %get-tuple-element.9.weight_ref, bf16[8,2,3584]{2,1,0:T(2,128)(2,1)S(1)} %all_to_all.11.rows_ref), custom_call_target="tpu_custom_call" | custom-call | tf_op jit(solution)/shard_map/combine/pallas_call | solution.py:118
Async XLA Ops:
  0.0 14.4 %copy-start = (bf16[1,3584,512]{2,1,0:T(8,128)(2,1)S(1)}, bf16[1,3584,512]{2,1,0:T(8,128)(2,1)}, u32[]{:S(2)}) copy-start(bf16[1,3584,512]{2,1,0:T(8,128)(2,1)} %gate_ref.1) | copy-start | bytes 11010052
  0.0 14.4 %copy-start.1 = (bf16[1,3584,512]{2,1,0:T(8,128)(2,1)S(1)}, bf16[1,3584,512]{2,1,0:T(8,128)(2,1)}, u32[]{:S(2)}) copy-start(bf16[1,3584,512]{2,1,0:T(8,128)(2,1)} %up_ref.1) | copy-start | bytes 11010052
  0.0 14.4 %copy-start.2 = (bf16[1,512,3584]{2,1,0:T(8,128)(2,1)S(1)}, bf16[1,512,3584]{2,1,0:T(8,128)(2,1)}, u32[]{:S(2)}) copy-start(bf16[1,512,3584]{2,1,0:T(8,128)(2,1)} %down_ref.1) | copy-start | bytes 11010052
  13.0 1.3 %collective-permute-start = (bf16[8,2,3584]{2,1,0:T(2,128)(2,1)S(1)}, bf16[8,2,3584]{2,1,0:T(2,128)(2,1)S(1)}, u32[]{:S(2)}, u32[]{:S(2)}) collective-permute-start(bf16[8,2,3584]{2,1,0:T(2,128)(2,1)S(1)} %all_to_all.10.own_ref), channel_id=1, source_target_pairs={{0,1},{1,0},{2,3},{3,2},{4,5},{5,4},{6,7},{7,6},{8,9},{9,8},{10,11... | collective-permute-start | bytes 344072 | tf_op jit(solution)/shard_map/ppermute | solution.py:100
  16.4 1.4 %collective-permute-start.1 = (bf16[8,2,3584]{2,1,0:T(2,128)(2,1)S(1)}, bf16[8,2,3584]{2,1,0:T(2,128)(2,1)S(1)}, u32[]{:S(2)}, u32[]{:S(2)}) collective-permute-start(bf16[8,2,3584]{2,1,0:T(2,128)(2,1)S(1)} %get-tuple-element.12), channel_id=1, source_target_pairs={{0,1},{1,0},{2,3},{3,2},{4,5},{5,4},{6,7},{7,6},{8,9},{9,8},{10,11... | collective-permute-start | bytes 344072 | tf_op jit(solution)/shard_map/ppermute | solution.py:113

commit v3 on v2

v3 whole, which is shorter than its diff:
```python
import functools
import jax
import jax.numpy as jnp
from jax import lax
from jax.experimental import pallas as pl
from jax.experimental.pallas import tpu as pltpu
from jax.sharding import PartitionSpec as P

SPLIT = 2
EXPERTS = 256


def slots_of(routes, slots, capacity, order):
    top, rows = routes.shape
    slot = lax.broadcasted_iota(jnp.int32, (slots, rows), 0)
    block, place = slot // capacity, slot % capacity
    expert = jnp.zeros_like(block)
    for j, chip in enumerate(order):
        expert = jnp.where(block == j, chip, expert)
    same = [routes[k : k + 1, :] == expert for k in range(top)]
    hit = functools.reduce(jnp.logical_or, same).astype(jnp.float32)
    earlier = lax.broadcasted_iota(jnp.int32, (rows, rows), 0) < lax.broadcasted_iota(
        jnp.int32, (rows, rows), 1
    )
    rank = jnp.dot(
        hit.astype(jnp.bfloat16), earlier.astype(jnp.bfloat16), preferred_element_type=jnp.float32
    )
    return jnp.where(rank == place.astype(jnp.float32), hit, 0.0), same


def route_kernel(
    capacity, order, routes_hbm, gates_hbm, tokens_hbm, out_ref, weight_ref, routes_v, gates_v, tokens_v, sems
):
    chips, halves, _, half = out_ref.shape
    parts = tokens_v.shape[0] // halves
    wide = half // parts
    routes_copy = pltpu.make_async_copy(routes_hbm, routes_v, sems.at[0])
    gates_copy = pltpu.make_async_copy(gates_hbm, gates_v, sems.at[1])
    token_copies = [
        pltpu.make_async_copy(tokens_hbm.at[:, pl.ds(i * wide, wide)], tokens_v.at[i], sems.at[2 + i])
        for i in range(halves * parts)
    ]
    routes_copy.start()
    for copy in token_copies:
        copy.start()
    gates_copy.start()
    routes_copy.wait()
    pick, same = slots_of(routes_v[...], chips * capacity, capacity, order)
    chosen = pick.astype(jnp.bfloat16)
    for i, copy in enumerate(token_copies):
        copy.wait()
        rows = jnp.dot(chosen, tokens_v[i], preferred_element_type=jnp.float32)
        part = slice(i % parts * wide, (i % parts + 1) * wide)
        out_ref[:, i // parts, :, part] = rows.astype(jnp.bfloat16).reshape(chips, capacity, wide)
    gates_copy.wait()
    gates = gates_v[...].astype(jnp.float32) / 256.0
    weight = jnp.zeros_like(pick)
    for k, hit in enumerate(same):
        weight = jnp.where(hit, gates[k : k + 1, :], weight)
    weight_ref[...] = (weight * pick).astype(jnp.bfloat16)


def flat(rows):
    return rows.reshape(rows.shape[0] * rows.shape[1], rows.shape[2])


def half_of(side, half):
    return pl.ds(pl.multiple_of(side * half, 128), half)


def enter_kernel(own_ref, gate_ref, up_ref, gate_out, up_out):
    half = own_ref.shape[2]
    mine = half_of(lax.axis_index("ep") % SPLIT, half)
    x = flat(own_ref[...])
    gate_out[...] = jnp.dot(x, gate_ref[0, mine, :], preferred_element_type=jnp.float32)
    up_out[...] = jnp.dot(x, up_ref[0, mine, :], preferred_element_type=jnp.float32)


def middle_kernel(other_ref, gate_acc, up_acc, gate_ref, up_ref, down_ref, hidden_ref, send_ref):
    half = other_ref.shape[2]
    theirs = half_of(1 - lax.axis_index("ep") % SPLIT, half)
    x = flat(other_ref[...])
    gate = gate_acc[...] + jnp.dot(x, gate_ref[0, theirs, :], preferred_element_type=jnp.float32)
    up = up_acc[...] + jnp.dot(x, up_ref[0, theirs, :], preferred_element_type=jnp.float32)
    hidden = (gate / (1.0 + jnp.exp(-gate)) * up).astype(jnp.bfloat16)
    hidden_ref[...] = hidden
    out = jnp.dot(hidden, down_ref[0, :, theirs], preferred_element_type=jnp.float32)
    send_ref[...] = out.astype(jnp.bfloat16).reshape(send_ref.shape)


def leave_kernel(hidden_ref, down_ref, keep_ref):
    half = keep_ref.shape[2]
    mine = half_of(lax.axis_index("ep") % SPLIT, half)
    out = jnp.dot(hidden_ref[...], down_ref[0, :, mine], preferred_element_type=jnp.float32)
    keep_ref[...] = out.reshape(keep_ref.shape)


def combine_kernel(weight_ref, rows_ref, out_hbm, out_v, sems):
    halves, half = rows_ref.shape[1], rows_ref.shape[3]
    parts = out_v.shape[0] // halves
    wide = half // parts
    copies = []
    for i in range(halves * parts):
        part = slice(i % parts * wide, (i % parts + 1) * wide)
        rows = flat(rows_ref[:, i // parts, :, part])
        out_v[i] = lax.dot_general(
            weight_ref[...], rows, (((0,), (0,)), ((), ())), preferred_element_type=jnp.float32
        ).astype(jnp.bfloat16)
        copies.append(
            pltpu.make_async_copy(out_v.at[i], out_hbm.at[:, pl.ds(i * wide, wide)], sems.at[i])
        )
        copies[-1].start()
    for copy in copies:
        copy.wait()


def group_order(chips):
    first = (5 * chips) // 8
    return [first] + [c for c in range(chips) if c != first]


VMEM = pl.BlockSpec(memory_space=pltpu.VMEM)
ANY = pl.BlockSpec(memory_space=pl.ANY)
LIMIT = pltpu.CompilerParams(vmem_limit_bytes=16 << 20)


def call(kernel, name, outs, *args, flops=0, **more):
    one = not isinstance(outs, tuple)
    options = dict(
        out_shape=outs,
        in_specs=[VMEM] * len(args),
        out_specs=VMEM if one else (VMEM,) * len(outs),
        name=name,
        compiler_params=LIMIT,
        cost_estimate=pl.CostEstimate(flops=flops, bytes_accessed=0, transcendentals=0),
    )
    return pl.pallas_call(kernel, **{**options, **more})(*args)


def shards(tokens, routes, gate_num, w_gate, w_up, w_down):
    tok_rows, top_count = routes.shape
    width = tokens.shape[1]
    hidden_width = w_gate.shape[2]
    devices = lax.axis_size("ep")
    chips = devices // SPLIT
    half = width // SPLIT
    capacity = max(2, min(tok_rows, 5 * tok_rows * top_count // (2 * EXPERTS)))
    order = group_order(chips)
    group = [[c * SPLIT + k for c in order for k in range(SPLIT)]]
    swap = [(d, d ^ 1) for d in range(devices)]
    slots, rows = chips * capacity, devices * capacity
    block = (devices, capacity, half)
    parts = 2 if half % 256 == 0 else 1
    bf16, f32 = jnp.bfloat16, jnp.float32
    shape = jax.ShapeDtypeStruct

    sources = [pltpu.with_memory_space_constraint(a, pltpu.HBM) for a in (routes.T, gate_num.T, tokens)]
    outgoing, weight = call(
        functools.partial(route_kernel, capacity, order),
        "route",
        (shape((chips, SPLIT, capacity, half), bf16), shape((slots, tok_rows), bf16)),
        *sources,
        flops=10**10,
        in_specs=[ANY] * 3,
        scratch_shapes=[
            pltpu.VMEM((top_count, tok_rows), jnp.int32),
            pltpu.VMEM((top_count, tok_rows), jnp.int32),
            pltpu.VMEM((SPLIT * parts, tok_rows, half // parts), bf16),
            pltpu.SemaphoreType.DMA((2 + SPLIT * parts,)),
        ],
    )
    exchange = functools.partial(
        lax.all_to_all,
        axis_name="ep",
        split_axis=0,
        concat_axis=0,
        tiled=True,
        axis_index_groups=group,
    )
    own = exchange(outgoing.reshape(block))
    other = lax.ppermute(own, "ep", swap)
    product = rows * half * hidden_width * 2
    accs = call(
        enter_kernel,
        "enter",
        (shape((rows, hidden_width), f32),) * 2,
        own,
        w_gate,
        w_up,
        flops=2 * product,
    )
    hidden, send = call(
        middle_kernel,
        "middle",
        (shape((rows, hidden_width), bf16), shape(block, bf16)),
        other,
        *accs,
        w_gate,
        w_up,
        w_down,
        flops=3 * product,
    )
    arrived = lax.ppermute(send, "ep", swap)
    keep = call(leave_kernel, "leave", shape(block, f32), hidden, w_down, flops=product)
    summed = (keep + arrived.astype(f32)).astype(bf16)
    returned = exchange(summed).reshape(chips, SPLIT, capacity, half)
    return call(
        combine_kernel,
        "combine",
        shape((tok_rows, width), bf16),
        weight,
        returned,
        out_specs=ANY,
        scratch_shapes=[
            pltpu.VMEM((SPLIT * parts, tok_rows, half // parts), bf16),
            pltpu.SemaphoreType.DMA((SPLIT * parts,)),
        ],
    )


def solution(mesh):
    return jax.shard_map(
        shards,
        mesh=mesh,
        in_specs=(
            P(("groups", "ep"), None),
            P(("groups", "ep"), None),
            P(("groups", "ep"), None),
            P("ep", None, None),
            P("ep", None, None),
            P("ep", None, None),
        ),
        out_specs=P(("groups", "ep"), None),
        check_vma=False,
    )
```

time: 28.2 us -> 27.6 us (0.979)
  waiting for transfers between devices: 2.5 us -> 0.77 us
  starting transfers between devices: 0.22 us -> 1.02 us
  blocking collectives: 20.8 us -> 20.1 us
  local copies, waits for them, and re-layouts: 0.01 us -> 0.6 us
  Pallas kernels: 4.39 us -> 4.78 us
    ppermute x1, waiting for transfers between devices: 1.32 us -> 0.23 us  [shards(): other = lax.ppermute(own, 'ep', swap)]
    all_to_all x2, blocking collectives: 20.8 us -> 20.1 us  [the longest x1 11.3 us: shards(): own = exchange(outgoing.reshape(block))]
    ppermute x1, waiting for transfers between devices: 1.18 us -> 0.53 us  [shards(): arrived = lax.ppermute(send, 'ep', swap)]
    unnamed x6, local copies, waits for them, and re-layouts: 0.01 us -> 0.6 us
    ppermute x1, starting transfers between devices: 0.01 us -> 0.48 us  [shards(): other = lax.ppermute(own, 'ep', swap)]
    pallas_call x3 -> x5, Pallas kernels: 4.39 us -> 4.78 us  [call(): return pl.pallas_call(kernel, **{**options, **more})(*args)]
    ppermute x1, starting transfers between devices: 0.21 us -> 0.54 us  [shards(): arrived = lax.ppermute(send, 'ep', swap)]
  transfers between devices with their start and end apart: 2 -> 2, of which waited for: 2 -> 2; matrix products, arithmetic and copies ran while one was open for 0% -> 0% of each run, Pallas kernels for 0% -> 4%
where the time goes in v3:
time: 27.6 us; the launch traced here: 27.4 us
  blocking collectives  20.1 us (73%)
  Pallas kernels  4.78 us (17%)
  starting transfers between devices  1.02 us (4%)
  waiting for transfers between devices  0.77 us (3%)
  local copies, waits for them, and re-layouts  0.6 us (2%)
    all_to_all x1, blocking collectives, shards(): own = exchange(outgoing.reshape(block))  11.3 us
    all_to_all x1, blocking collectives, shards(): returned = exchange(summed).reshape(chips, SPLIT, capacity, half)  8.73 us
    pallas_call x5, Pallas kernels, call(): return pl.pallas_call(kernel, **{**options, **more})(*args)  4.78 us
    unnamed x6, local copies, waits for them, and re-layouts  0.6 us
  transfers between devices with their start and end apart: 2, of which 2 were waited for; matrix products, arithmetic and copies ran while one was open for 0% of the time, Pallas kernels for 4%

profile of v3, /device:TPU:0, one launch (start us, length us, event | category | flops | bytes accessed | tf_op | source)
XLA Modules:
  0.0 27.4 jit_solution(6798993633598669234)
XLA Ops:
  0.0 0.0 copy-start
  0.0 0.0 copy-start.1
  0.0 1.6 %route.1 = (bf16[8,2,2,1792]{3,2,1,0:T(2,128)(2,1)S(1)}, bf16[16,32]{1,0:T(8,128)(2,1)S(1)}) custom-call(s32[8,32]{1,0:T(8,128)} %bitcast.6, s32[8,32]{1,0:T(8,128)} %bitcast.7, bf16[32,3584]{1,0:T(8,128)(2,1)} %tokens_hbm.1), custom_call_target="tpu_custom_call" | custom-call | flops 10000000000 | tf_op jit(solution)/shard_map/route/pallas_call | solution.py:137
  1.6 11.3 %all_to_all.10.own_ref = bf16[16,2,1792]{2,1,0:T(2,128)(2,1)S(1)} all-to-all(bf16[16,2,1792]{2,1,0:T(2,128)(2,1)S(1)} %bitcast.5), channel_id=1, replica_groups={{10,11,0,1,2,3,4,5,6,7,8,9,12,13,14,15},{26,27,16,17,18,19,20,21,22,23,..., dimensions={0} | all-to-all | bytes 229376 | tf_op jit(solution)/shard_map/all_to_all | solution.py:180
  12.9 0.0 copy-start.2
  12.9 0.5 %collective-permute-start = (bf16[16,2,1792]{2,1,0:T(2,128)(2,1)S(1)}, bf16[16,2,1792]{2,1,0:T(2,128)(2,1)S(1)}, u32[]{:S(2)}, u32[]{:S(2)}) collective-permute-start(bf16[16,2,1792]{2,1,0:T(2,128)(2,1)S(1)} %all_to_all.10.own_ref), channel_id=1, source_target_pairs={{0,1},{1,0},{2,3},{3,2},{4,5},{5,4},{6,7},{7,6},{8,9},{9,8},{10,11... | collective-permute-start | bytes 344072 | tf_op jit(solution)/shard_map/ppermute | solution.py:181
  13.4 0.0 copy-done
  13.4 0.0 copy-done.1
  13.4 0.7 %enter.1 = (f32[32,512]{1,0:T(8,128)S(1)}, f32[32,512]{1,0:T(8,128)S(1)}) custom-call(bf16[16,2,1792]{2,1,0:T(2,128)(2,1)S(1)} %all_to_all.10.own_ref, bf16[1,3584,512]{2,1,0:T(8,128)(2,1)S(1)} %copy-done, bf16[1,3584,512]{2,1,0:T(8,128)(2,1)S(1)} %copy-done.1), custom_call_target="tpu_custom_call" | custom-call | flops 117440512 | tf_op jit(solution)/shard_map/enter/pallas_call | solution.py:137
  14.1 0.2 collective-permute-done.other_ref
  14.4 0.6 %copy-done.2 = bf16[1,512,3584]{2,1,0:T(8,128)(2,1)S(1)} copy-done((bf16[1,512,3584]{2,1,0:T(8,128)(2,1)S(1)}, bf16[1,512,3584]{2,1,0:T(8,128)(2,1)}, u32[]{:S(2)}) %copy-start.2) | copy-done | bytes 3670040
  14.9 1.2 %middle.1 = (bf16[32,512]{1,0:T(8,128)(2,1)S(1)}, bf16[16,2,1792]{2,1,0:T(2,128)(2,1)S(1)}) custom-call(bf16[16,2,1792]{2,1,0:T(2,128)(2,1)S(1)} %collective-permute-done.other_ref, f32[32,512]{1,0:T(8,128)S(1)} %get-tuple-element.13.gate_acc, f32[32,512]{1,0:T(8,128)S(1)} %get-tuple-element.14.up_acc, bf16[1,3584,512]{2,1,0:T(8,128)(2,1)S(1)} %copy-done, ...), custom_call_target="tpu_custom_call" | custom-call | flops 176160768 | tf_op jit(solution)/shard_map/middle/pallas_call | solution.py:137
  16.1 0.5 %collective-permute-start.1 = (bf16[16,2,1792]{2,1,0:T(2,128)(2,1)S(1)}, bf16[16,2,1792]{2,1,0:T(2,128)(2,1)S(1)}, u32[]{:S(2)}, u32[]{:S(2)}) collective-permute-start(bf16[16,2,1792]{2,1,0:T(2,128)(2,1)S(1)} %get-tuple-element.16), channel_id=1, source_target_pairs={{0,1},{1,0},{2,3},{3,2},{4,5},{5,4},{6,7},{7,6},{8,9},{9,8},{10,11... | collective-permute-start | bytes 344072 | tf_op jit(solution)/shard_map/ppermute | solution.py:203
  16.7 0.4 %leave.1 = f32[16,2,1792]{2,1,0:T(2,128)S(1)} custom-call(bf16[32,512]{1,0:T(8,128)(2,1)S(1)} %get-tuple-element.15.hidden_ref, bf16[1,512,3584]{2,1,0:T(8,128)(2,1)S(1)} %copy-done.2), custom_call_target="tpu_custom_call" | custom-call | flops 58720256 | tf_op jit(solution)/shard_map/leave/pallas_call | solution.py:137
  17.1 0.5 %collective-permute-done.1 = bf16[16,2,1792]{2,1,0:T(2,128)(2,1)S(1)} collective-permute-done((bf16[16,2,1792]{2,1,0:T(2,128)(2,1)S(1)}, bf16[16,2,1792]{2,1,0:T(2,128)(2,1)S(1)}, u32[]{:S(2)}, u32[]{:S(2)}) %collective-permute-start.1) | collective-permute-done | bytes 114720 | tf_op jit(solution)/shard_map/ppermute | solution.py:203
  17.6 0.1 add_convert_fusion
  17.7 8.7 %all_to_all.11 = bf16[16,2,1792]{2,1,0:T(2,128)(2,1)S(1)} all-to-all(bf16[16,2,1792]{2,1,0:T(2,128)(2,1)S(1)} %add_convert_fusion), channel_id=1, replica_groups={{10,11,0,1,2,3,4,5,6,7,8,9,12,13,14,15},{26,27,16,17,18,19,20,21,22,23,..., dimensions={0} | all-to-all | bytes 229376 | tf_op jit(solution)/shard_map/all_to_all | solution.py:206
  26.5 0.9 %combine.1 = bf16[32,3584]{1,0:T(8,128)(2,1)} custom-call(bf16[16,32]{1,0:T(8,128)(2,1)S(1)} %get-tuple-element.11.weight_ref, bf16[8,2,2,1792]{3,2,1,0:T(2,128)(2,1)S(1)} %bitcast.4), custom_call_target="tpu_custom_call" | custom-call | tf_op jit(solution)/shard_map/combine/pallas_call | solution.py:137
Async XLA Ops:
  0.0 13.4 %copy-start = (bf16[1,3584,512]{2,1,0:T(8,128)(2,1)S(1)}, bf16[1,3584,512]{2,1,0:T(8,128)(2,1)}, u32[]{:S(2)}) copy-start(bf16[1,3584,512]{2,1,0:T(8,128)(2,1)} %gate_ref.3) | copy-start | bytes 11010052
  0.0 13.4 %copy-start.1 = (bf16[1,3584,512]{2,1,0:T(8,128)(2,1)S(1)}, bf16[1,3584,512]{2,1,0:T(8,128)(2,1)}, u32[]{:S(2)}) copy-start(bf16[1,3584,512]{2,1,0:T(8,128)(2,1)} %up_ref.3) | copy-start | bytes 11010052
  12.9 2.0 %copy-start.2 = (bf16[1,512,3584]{2,1,0:T(8,128)(2,1)S(1)}, bf16[1,512,3584]{2,1,0:T(8,128)(2,1)}, u32[]{:S(2)}) copy-start(bf16[1,512,3584]{2,1,0:T(8,128)(2,1)} %down_ref.3) | copy-start | bytes 11010052
  12.9 1.4 %collective-permute-start = (bf16[16,2,1792]{2,1,0:T(2,128)(2,1)S(1)}, bf16[16,2,1792]{2,1,0:T(2,128)(2,1)S(1)}, u32[]{:S(2)}, u32[]{:S(2)}) collective-permute-start(bf16[16,2,1792]{2,1,0:T(2,128)(2,1)S(1)} %all_to_all.10.own_ref), channel_id=1, source_target_pairs={{0,1},{1,0},{2,3},{3,2},{4,5},{5,4},{6,7},{7,6},{8,9},{9,8},{10,11... | collective-permute-start | bytes 344072 | tf_op jit(solution)/shard_map/ppermute | solution.py:181
  16.1 1.5 %collective-permute-start.1 = (bf16[16,2,1792]{2,1,0:T(2,128)(2,1)S(1)}, bf16[16,2,1792]{2,1,0:T(2,128)(2,1)S(1)}, u32[]{:S(2)}, u32[]{:S(2)}) collective-permute-start(bf16[16,2,1792]{2,1,0:T(2,128)(2,1)S(1)} %get-tuple-element.16), channel_id=1, source_target_pairs={{0,1},{1,0},{2,3},{3,2},{4,5},{5,4},{6,7},{7,6},{8,9},{9,8},{10,11... | collective-permute-start | bytes 344072 | tf_op jit(solution)/shard_map/ppermute | solution.py:203

commit v4 on v3

--- a/solution.py
+++ b/solution.py
@@ -32,32 +32,33 @@
     capacity, order, routes_hbm, gates_hbm, tokens_hbm, out_ref, weight_ref, routes_v, gates_v, tokens_v, sems
 ):
     chips, halves, _, half = out_ref.shape
-    parts = tokens_v.shape[0] // halves
-    wide = half // parts
-    routes_copy = pltpu.make_async_copy(routes_hbm, routes_v, sems.at[0])
-    gates_copy = pltpu.make_async_copy(gates_hbm, gates_v, sems.at[1])
-    token_copies = [
-        pltpu.make_async_copy(tokens_hbm.at[:, pl.ds(i * wide, wide)], tokens_v.at[i], sems.at[2 + i])
-        for i in range(halves * parts)
+    copies = [
+        pltpu.make_async_copy(source, target, sems.at[i])
+        for i, (source, target) in enumerate(
+            ((routes_hbm, routes_v), (tokens_hbm, tokens_v), (gates_hbm, gates_v))
+        )
     ]
-    routes_copy.start()
-    for copy in token_copies:
+    for copy in copies:
         copy.start()
-    gates_copy.start()
-    routes_copy.wait()
+    copies[0].wait()
     pick, same = slots_of(routes_v[...], chips * capacity, capacity, order)
-    chosen = pick.astype(jnp.bfloat16)
-    for i, copy in enumerate(token_copies):
-        copy.wait()
-        rows = jnp.dot(chosen, tokens_v[i], preferred_element_type=jnp.float32)
-        part = slice(i % parts * wide, (i % parts + 1) * wide)
-        out_ref[:, i // parts, :, part] = rows.astype(jnp.bfloat16).reshape(chips, capacity, wide)
-    gates_copy.wait()
+    copies[2].wait()
     gates = gates_v[...].astype(jnp.float32) / 256.0
     weight = jnp.zeros_like(pick)
     for k, hit in enumerate(same):
         weight = jnp.where(hit, gates[k : k + 1, :], weight)
     weight_ref[...] = (weight * pick).astype(jnp.bfloat16)
+    copies[1].wait()
+    rows = jnp.dot(
+        pick.astype(jnp.bfloat16), tokens_v[...], preferred_element_type=jnp.float32
+    ).astype(jnp.bfloat16)
+    for k in range(halves):
+        part = rows[:, k * half : (k + 1) * half]
+        out_ref[:, k] = part.reshape(chips, capacity, half)
+
+
+def mark_kernel(in_ref, out_ref):
+    del in_ref, out_ref
 
 
 def flat(rows):
@@ -68,7 +69,8 @@
     return pl.ds(pl.multiple_of(side * half, 128), half)
 
 
-def enter_kernel(own_ref, gate_ref, up_ref, gate_out, up_out):
+def enter_kernel(own_ref, gate_ref, up_ref, down_ref, gate_out, up_out):
+    del down_ref
     half = own_ref.shape[2]
     mine = half_of(lax.axis_index("ep") % SPLIT, half)
     x = flat(own_ref[...])
@@ -160,14 +162,17 @@
         "route",
         (shape((chips, SPLIT, capacity, half), bf16), shape((slots, tok_rows), bf16)),
         *sources,
-        flops=10**10,
         in_specs=[ANY] * 3,
         scratch_shapes=[
             pltpu.VMEM((top_count, tok_rows), jnp.int32),
             pltpu.VMEM((top_count, tok_rows), jnp.int32),
-            pltpu.VMEM((SPLIT * parts, tok_rows, half // parts), bf16),
-            pltpu.SemaphoreType.DMA((2 + SPLIT * parts,)),
+            pltpu.VMEM((tok_rows, width), bf16),
+            pltpu.SemaphoreType.DMA((3,)),
         ],
+    )
+    outgoing = outgoing.reshape(block)
+    outgoing = call(
+        mark_kernel, "mark", shape(block, bf16), outgoing, flops=10**10, input_output_aliases={0: 0}
     )
     exchange = functools.partial(
         lax.all_to_all,
@@ -177,7 +182,7 @@
         tiled=True,
         axis_index_groups=group,
     )
-    own = exchange(outgoing.reshape(block))
+    own = exchange(outgoing)
     other = lax.ppermute(own, "ep", swap)
     product = rows * half * hidden_width * 2
     accs = call(
@@ -187,6 +192,7 @@
         own,
         w_gate,
         w_up,
+        w_down,
         flops=2 * product,
     )
     hidden, send = call(

time: 27.6 us -> 26.7 us (0.967)
  local copies, waits for them, and re-layouts: 0.6 us -> 0.02 us
  Pallas kernels: 4.78 us -> 4.35 us
    unnamed x6, local copies, waits for them, and re-layouts: 0.6 us -> 0.02 us
    pallas_call x5 -> x6, Pallas kernels: 4.78 us -> 4.35 us  [call(): return pl.pallas_call(kernel, **{**options, **more})(*args)]
where the time goes in v4:
time: 26.7 us; the launch traced here: 26.4 us
  blocking collectives  20.2 us (76%)
  Pallas kernels  4.35 us (16%)
  starting transfers between devices  0.9 us (3%)
  waiting for transfers between devices  0.76 us (3%)
    all_to_all x1, blocking collectives, shards(): own = exchange(outgoing)  11.5 us
    all_to_all x1, blocking collectives, shards(): returned = exchange(summed).reshape(chips, SPLIT, capacity, half)  8.66 us
    pallas_call x6, Pallas kernels, call(): return pl.pallas_call(kernel, **{**options, **more})(*args)  4.35 us
  transfers between devices with their start and end apart: 2, of which 2 were waited for; matrix products, arithmetic and copies ran while one was open for 0% of the time, Pallas kernels for 4%

profile of v4, /device:TPU:0, one launch (start us, length us, event | category | flops | bytes accessed | tf_op | source)
XLA Modules:
  0.0 26.4 jit_solution(11384930604735999468)
XLA Ops:
  0.0 1.1 %route.1 = (bf16[8,2,2,1792]{3,2,1,0:T(2,128)(2,1)S(1)}, bf16[16,32]{1,0:T(8,128)(2,1)S(1)}) custom-call(s32[8,32]{1,0:T(8,128)} %bitcast.6, s32[8,32]{1,0:T(8,128)} %bitcast.7, bf16[32,3584]{1,0:T(8,128)(2,1)} %tokens_hbm.1), custom_call_target="tpu_custom_call" | custom-call | tf_op jit(solution)/shard_map/route/pallas_call | solution.py:139
  1.2 0.0 copy-start
  1.2 0.0 copy-start.1
  1.2 0.0 copy-start.2
  1.2 11.5 %all_to_all.10.own_ref = bf16[16,2,1792]{2,1,0:T(2,128)(2,1)S(1)} all-to-all(bf16[16,2,1792]{2,1,0:T(2,128)(2,1)S(1)} %mark.1), channel_id=1, replica_groups={{10,11,0,1,2,3,4,5,6,7,8,9,12,13,14,15},{26,27,16,17,18,19,20,21,22,23,..., dimensions={0} | all-to-all | bytes 229376 | tf_op jit(solution)/shard_map/all_to_all | solution.py:185
  12.7 0.5 %collective-permute-start = (bf16[16,2,1792]{2,1,0:T(2,128)(2,1)S(1)}, bf16[16,2,1792]{2,1,0:T(2,128)(2,1)S(1)}, u32[]{:S(2)}, u32[]{:S(2)}) collective-permute-start(bf16[16,2,1792]{2,1,0:T(2,128)(2,1)S(1)} %all_to_all.10.own_ref), channel_id=1, source_target_pairs={{0,1},{1,0},{2,3},{3,2},{4,5},{5,4},{6,7},{7,6},{8,9},{9,8},{10,11... | collective-permute-start | bytes 344072 | tf_op jit(solution)/shard_map/ppermute | solution.py:186
  13.2 0.0 copy-done
  13.2 0.0 copy-done.1
  13.2 0.0 copy-done.2
  13.2 0.7 %enter.1 = (f32[32,512]{1,0:T(8,128)S(1)}, f32[32,512]{1,0:T(8,128)S(1)}) custom-call(bf16[16,2,1792]{2,1,0:T(2,128)(2,1)S(1)} %all_to_all.10.own_ref, bf16[1,3584,512]{2,1,0:T(8,128)(2,1)S(1)} %copy-done.1, bf16[1,3584,512]{2,1,0:T(8,128)(2,1)S(1)} %copy-done.2, bf16[1,512,3584]{2,1,0:T(8,128)(2,1)S(1)} %copy-done), custom_call_target="tpu_custom_call" | custom-call | flops 117440512 | tf_op jit(solution)/shard_map/enter/pallas_call | solution.py:139
  13.9 0.2 collective-permute-done.other_ref
  14.2 1.2 %middle.1 = (bf16[32,512]{1,0:T(8,128)(2,1)S(1)}, bf16[16,2,1792]{2,1,0:T(2,128)(2,1)S(1)}) custom-call(bf16[16,2,1792]{2,1,0:T(2,128)(2,1)S(1)} %collective-permute-done.other_ref, f32[32,512]{1,0:T(8,128)S(1)} %get-tuple-element.13.gate_acc, f32[32,512]{1,0:T(8,128)S(1)} %get-tuple-element.14.up_acc, bf16[1,3584,512]{2,1,0:T(8,128)(2,1)S(1)} %copy-done.1, ...), custom_call_target="tpu_custom_call" | custom-call | flops 176160768 | tf_op jit(solution)/shard_map/middle/pallas_call | solution.py:139
  15.3 0.4 %collective-permute-start.1 = (bf16[16,2,1792]{2,1,0:T(2,128)(2,1)S(1)}, bf16[16,2,1792]{2,1,0:T(2,128)(2,1)S(1)}, u32[]{:S(2)}, u32[]{:S(2)}) collective-permute-start(bf16[16,2,1792]{2,1,0:T(2,128)(2,1)S(1)} %get-tuple-element.16), channel_id=1, source_target_pairs={{0,1},{1,0},{2,3},{3,2},{4,5},{5,4},{6,7},{7,6},{8,9},{9,8},{10,11... | collective-permute-start | bytes 344072 | tf_op jit(solution)/shard_map/ppermute | solution.py:209
  15.8 0.4 %leave.1 = f32[16,2,1792]{2,1,0:T(2,128)S(1)} custom-call(bf16[32,512]{1,0:T(8,128)(2,1)S(1)} %get-tuple-element.15.hidden_ref, bf16[1,512,3584]{2,1,0:T(8,128)(2,1)S(1)} %copy-done), custom_call_target="tpu_custom_call" | custom-call | flops 58720256 | tf_op jit(solution)/shard_map/leave/pallas_call | solution.py:139
  16.2 0.5 %collective-permute-done.1 = bf16[16,2,1792]{2,1,0:T(2,128)(2,1)S(1)} collective-permute-done((bf16[16,2,1792]{2,1,0:T(2,128)(2,1)S(1)}, bf16[16,2,1792]{2,1,0:T(2,128)(2,1)S(1)}, u32[]{:S(2)}, u32[]{:S(2)}) %collective-permute-start.1) | collective-permute-done | bytes 114720 | tf_op jit(solution)/shard_map/ppermute | solution.py:209
  16.7 0.1 add_convert_fusion
  16.9 8.7 %all_to_all.11 = bf16[16,2,1792]{2,1,0:T(2,128)(2,1)S(1)} all-to-all(bf16[16,2,1792]{2,1,0:T(2,128)(2,1)S(1)} %add_convert_fusion), channel_id=1, replica_groups={{10,11,0,1,2,3,4,5,6,7,8,9,12,13,14,15},{26,27,16,17,18,19,20,21,22,23,..., dimensions={0} | all-to-all | bytes 229376 | tf_op jit(solution)/shard_map/all_to_all | solution.py:212
  25.5 0.9 %combine.1 = bf16[32,3584]{1,0:T(8,128)(2,1)} custom-call(bf16[16,32]{1,0:T(8,128)(2,1)S(1)} %get-tuple-element.11.weight_ref, bf16[8,2,2,1792]{3,2,1,0:T(2,128)(2,1)S(1)} %bitcast.4), custom_call_target="tpu_custom_call" | custom-call | tf_op jit(solution)/shard_map/combine/pallas_call | solution.py:139
  (1 shorter events, 0.0 us)
Async XLA Ops:
  1.2 12.1 %copy-start = (bf16[1,512,3584]{2,1,0:T(8,128)(2,1)S(1)}, bf16[1,512,3584]{2,1,0:T(8,128)(2,1)}, u32[]{:S(2)}) copy-start(bf16[1,512,3584]{2,1,0:T(8,128)(2,1)} %down_ref.5) | copy-start | bytes 11010052
  1.2 12.1 %copy-start.1 = (bf16[1,3584,512]{2,1,0:T(8,128)(2,1)S(1)}, bf16[1,3584,512]{2,1,0:T(8,128)(2,1)}, u32[]{:S(2)}) copy-start(bf16[1,3584,512]{2,1,0:T(8,128)(2,1)} %gate_ref.3) | copy-start | bytes 11010052
  1.2 12.0 %copy-start.2 = (bf16[1,3584,512]{2,1,0:T(8,128)(2,1)S(1)}, bf16[1,3584,512]{2,1,0:T(8,128)(2,1)}, u32[]{:S(2)}) copy-start(bf16[1,3584,512]{2,1,0:T(8,128)(2,1)} %up_ref.3) | copy-start | bytes 11010052
  12.7 1.4 %collective-permute-start = (bf16[16,2,1792]{2,1,0:T(2,128)(2,1)S(1)}, bf16[16,2,1792]{2,1,0:T(2,128)(2,1)S(1)}, u32[]{:S(2)}, u32[]{:S(2)}) collective-permute-start(bf16[16,2,1792]{2,1,0:T(2,128)(2,1)S(1)} %all_to_all.10.own_ref), channel_id=1, source_target_pairs={{0,1},{1,0},{2,3},{3,2},{4,5},{5,4},{6,7},{7,6},{8,9},{9,8},{10,11... | collective-permute-start | bytes 344072 | tf_op jit(solution)/shard_map/ppermute | solution.py:186
  15.3 1.4 %collective-permute-start.1 = (bf16[16,2,1792]{2,1,0:T(2,128)(2,1)S(1)}, bf16[16,2,1792]{2,1,0:T(2,128)(2,1)S(1)}, u32[]{:S(2)}, u32[]{:S(2)}) collective-permute-start(bf16[16,2,1792]{2,1,0:T(2,128)(2,1)S(1)} %get-tuple-element.16), channel_id=1, source_target_pairs={{0,1},{1,0},{2,3},{3,2},{4,5},{5,4},{6,7},{7,6},{8,9},{9,8},{10,11... | collective-permute-start | bytes 344072 | tf_op jit(solution)/shard_map/ppermute | solution.py:209

commit v5 on v4

--- a/solution.py
+++ b/solution.py
@@ -54,7 +54,7 @@
     ).astype(jnp.bfloat16)
     for k in range(halves):
         part = rows[:, k * half : (k + 1) * half]
-        out_ref[:, k] = part.reshape(chips, capacity, half)
+        out_ref[:, halves - 1 - k] = part.reshape(chips, capacity, half)
 
 
 def mark_kernel(in_ref, out_ref):
@@ -104,7 +104,7 @@
     copies = []
     for i in range(halves * parts):
         part = slice(i % parts * wide, (i % parts + 1) * wide)
-        rows = flat(rows_ref[:, i // parts, :, part])
+        rows = flat(rows_ref[:, halves - 1 - i // parts, :, part])
         out_v[i] = lax.dot_general(
             weight_ref[...], rows, (((0,), (0,)), ((), ())), preferred_element_type=jnp.float32
         ).astype(jnp.bfloat16)
@@ -148,7 +148,7 @@
     half = width // SPLIT
     capacity = max(2, min(tok_rows, 5 * tok_rows * top_count // (2 * EXPERTS)))
     order = group_order(chips)
-    group = [[c * SPLIT + k for c in order for k in range(SPLIT)]]
+    group = [[c * SPLIT + k for c in order for k in reversed(range(SPLIT))]]
     swap = [(d, d ^ 1) for d in range(devices)]
     slots, rows = chips * capacity, devices * capacity
     block = (devices, capacity, half)

time: 26.7 us -> 26.3 us (0.985)
  blocking collectives: 20.2 us -> 19.8 us
    all_to_all x1, blocking collectives: 11.5 us -> 11.2 us  [shards(): own = exchange(outgoing)]
where the time goes in v5:
time: 26.3 us; the launch traced here: 26 us
  blocking collectives  19.8 us (75%)
  Pallas kernels  4.35 us (17%)
  starting transfers between devices  0.9 us (3%)
  waiting for transfers between devices  0.76 us (3%)
    all_to_all x1, blocking collectives, shards(): own = exchange(outgoing)  11.2 us
    all_to_all x1, blocking collectives, shards(): returned = exchange(summed).reshape(chips, SPLIT, capacity, half)  8.62 us
    pallas_call x6, Pallas kernels, call(): return pl.pallas_call(kernel, **{**options, **more})(*args)  4.35 us
    ppermute x1, waiting for transfers between devices, shards(): arrived = lax.ppermute(send, 'ep', swap)  0.53 us
  transfers between devices with their start and end apart: 2, of which 2 were waited for; matrix products, arithmetic and copies ran while one was open for 0% of the time, Pallas kernels for 4%

profile of v5, /device:TPU:0, one launch (start us, length us, event | category | flops | bytes accessed | tf_op | source)
XLA Modules:
  0.0 26.0 jit_solution(6249782316437845728)
XLA Ops:
  0.0 1.1 %route.1 = (bf16[8,2,2,1792]{3,2,1,0:T(2,128)(2,1)S(1)}, bf16[16,32]{1,0:T(8,128)(2,1)S(1)}) custom-call(s32[8,32]{1,0:T(8,128)} %bitcast.6, s32[8,32]{1,0:T(8,128)} %bitcast.7, bf16[32,3584]{1,0:T(8,128)(2,1)} %tokens_hbm.1), custom_call_target="tpu_custom_call" | custom-call | tf_op jit(solution)/shard_map/route/pallas_call | solution.py:139
  1.2 0.0 copy-start
  1.2 0.0 copy-start.1
  1.2 0.0 copy-start.2
  1.2 11.2 %all_to_all.10.own_ref = bf16[16,2,1792]{2,1,0:T(2,128)(2,1)S(1)} all-to-all(bf16[16,2,1792]{2,1,0:T(2,128)(2,1)S(1)} %mark.1), channel_id=1, replica_groups={{11,10,1,0,3,2,5,4,7,6,9,8,13,12,15,14},{27,26,17,16,19,18,21,20,23,22,..., dimensions={0} | all-to-all | bytes 229376 | tf_op jit(solution)/shard_map/all_to_all | solution.py:185
  12.4 0.5 %collective-permute-start = (bf16[16,2,1792]{2,1,0:T(2,128)(2,1)S(1)}, bf16[16,2,1792]{2,1,0:T(2,128)(2,1)S(1)}, u32[]{:S(2)}, u32[]{:S(2)}) collective-permute-start(bf16[16,2,1792]{2,1,0:T(2,128)(2,1)S(1)} %all_to_all.10.own_ref), channel_id=1, source_target_pairs={{0,1},{1,0},{2,3},{3,2},{4,5},{5,4},{6,7},{7,6},{8,9},{9,8},{10,11... | collective-permute-start | bytes 344072 | tf_op jit(solution)/shard_map/ppermute | solution.py:186
  12.8 0.0 copy-done
  12.9 0.0 copy-done.1
  12.9 0.0 copy-done.2
  12.9 0.7 %enter.1 = (f32[32,512]{1,0:T(8,128)S(1)}, f32[32,512]{1,0:T(8,128)S(1)}) custom-call(bf16[16,2,1792]{2,1,0:T(2,128)(2,1)S(1)} %all_to_all.10.own_ref, bf16[1,3584,512]{2,1,0:T(8,128)(2,1)S(1)} %copy-done.1, bf16[1,3584,512]{2,1,0:T(8,128)(2,1)S(1)} %copy-done.2, bf16[1,512,3584]{2,1,0:T(8,128)(2,1)S(1)} %copy-done), custom_call_target="tpu_custom_call" | custom-call | flops 117440512 | tf_op jit(solution)/shard_map/enter/pallas_call | solution.py:139
  13.6 0.2 collective-permute-done.other_ref
  13.8 1.2 %middle.1 = (bf16[32,512]{1,0:T(8,128)(2,1)S(1)}, bf16[16,2,1792]{2,1,0:T(2,128)(2,1)S(1)}) custom-call(bf16[16,2,1792]{2,1,0:T(2,128)(2,1)S(1)} %collective-permute-done.other_ref, f32[32,512]{1,0:T(8,128)S(1)} %get-tuple-element.13.gate_acc, f32[32,512]{1,0:T(8,128)S(1)} %get-tuple-element.14.up_acc, bf16[1,3584,512]{2,1,0:T(8,128)(2,1)S(1)} %copy-done.1, ...), custom_call_target="tpu_custom_call" | custom-call | flops 176160768 | tf_op jit(solution)/shard_map/middle/pallas_call | solution.py:139
  15.0 0.4 %collective-permute-start.1 = (bf16[16,2,1792]{2,1,0:T(2,128)(2,1)S(1)}, bf16[16,2,1792]{2,1,0:T(2,128)(2,1)S(1)}, u32[]{:S(2)}, u32[]{:S(2)}) collective-permute-start(bf16[16,2,1792]{2,1,0:T(2,128)(2,1)S(1)} %get-tuple-element.16), channel_id=1, source_target_pairs={{0,1},{1,0},{2,3},{3,2},{4,5},{5,4},{6,7},{7,6},{8,9},{9,8},{10,11... | collective-permute-start | bytes 344072 | tf_op jit(solution)/shard_map/ppermute | solution.py:209
  15.4 0.4 %leave.1 = f32[16,2,1792]{2,1,0:T(2,128)S(1)} custom-call(bf16[32,512]{1,0:T(8,128)(2,1)S(1)} %get-tuple-element.15.hidden_ref, bf16[1,512,3584]{2,1,0:T(8,128)(2,1)S(1)} %copy-done), custom_call_target="tpu_custom_call" | custom-call | flops 58720256 | tf_op jit(solution)/shard_map/leave/pallas_call | solution.py:139
  15.8 0.5 %collective-permute-done.1 = bf16[16,2,1792]{2,1,0:T(2,128)(2,1)S(1)} collective-permute-done((bf16[16,2,1792]{2,1,0:T(2,128)(2,1)S(1)}, bf16[16,2,1792]{2,1,0:T(2,128)(2,1)S(1)}, u32[]{:S(2)}, u32[]{:S(2)}) %collective-permute-start.1) | collective-permute-done | bytes 114720 | tf_op jit(solution)/shard_map/ppermute | solution.py:209
  16.4 0.1 add_convert_fusion
  16.5 8.6 %all_to_all.11 = bf16[16,2,1792]{2,1,0:T(2,128)(2,1)S(1)} all-to-all(bf16[16,2,1792]{2,1,0:T(2,128)(2,1)S(1)} %add_convert_fusion), channel_id=1, replica_groups={{11,10,1,0,3,2,5,4,7,6,9,8,13,12,15,14},{27,26,17,16,19,18,21,20,23,22,..., dimensions={0} | all-to-all | bytes 229376 | tf_op jit(solution)/shard_map/all_to_all | solution.py:212
  25.1 0.9 %combine.1 = bf16[32,3584]{1,0:T(8,128)(2,1)} custom-call(bf16[16,32]{1,0:T(8,128)(2,1)S(1)} %get-tuple-element.11.weight_ref, bf16[8,2,2,1792]{3,2,1,0:T(2,128)(2,1)S(1)} %bitcast.4), custom_call_target="tpu_custom_call" | custom-call | tf_op jit(solution)/shard_map/combine/pallas_call | solution.py:139
  (1 shorter events, 0.0 us)
Async XLA Ops:
  1.2 11.7 %copy-start = (bf16[1,512,3584]{2,1,0:T(8,128)(2,1)S(1)}, bf16[1,512,3584]{2,1,0:T(8,128)(2,1)}, u32[]{:S(2)}) copy-start(bf16[1,512,3584]{2,1,0:T(8,128)(2,1)} %down_ref.5) | copy-start | bytes 11010052
  1.2 11.7 %copy-start.1 = (bf16[1,3584,512]{2,1,0:T(8,128)(2,1)S(1)}, bf16[1,3584,512]{2,1,0:T(8,128)(2,1)}, u32[]{:S(2)}) copy-start(bf16[1,3584,512]{2,1,0:T(8,128)(2,1)} %gate_ref.3) | copy-start | bytes 11010052
  1.2 11.7 %copy-start.2 = (bf16[1,3584,512]{2,1,0:T(8,128)(2,1)S(1)}, bf16[1,3584,512]{2,1,0:T(8,128)(2,1)}, u32[]{:S(2)}) copy-start(bf16[1,3584,512]{2,1,0:T(8,128)(2,1)} %up_ref.3) | copy-start | bytes 11010052
  12.4 1.4 %collective-permute-start = (bf16[16,2,1792]{2,1,0:T(2,128)(2,1)S(1)}, bf16[16,2,1792]{2,1,0:T(2,128)(2,1)S(1)}, u32[]{:S(2)}, u32[]{:S(2)}) collective-permute-start(bf16[16,2,1792]{2,1,0:T(2,128)(2,1)S(1)} %all_to_all.10.own_ref), channel_id=1, source_target_pairs={{0,1},{1,0},{2,3},{3,2},{4,5},{5,4},{6,7},{7,6},{8,9},{9,8},{10,11... | collective-permute-start | bytes 344072 | tf_op jit(solution)/shard_map/ppermute | solution.py:186
  15.0 1.4 %collective-permute-start.1 = (bf16[16,2,1792]{2,1,0:T(2,128)(2,1)S(1)}, bf16[16,2,1792]{2,1,0:T(2,128)(2,1)S(1)}, u32[]{:S(2)}, u32[]{:S(2)}) collective-permute-start(bf16[16,2,1792]{2,1,0:T(2,128)(2,1)S(1)} %get-tuple-element.16), channel_id=1, source_target_pairs={{0,1},{1,0},{2,3},{3,2},{4,5},{5,4},{6,7},{7,6},{8,9},{9,8},{10,11... | collective-permute-start | bytes 344072 | tf_op jit(solution)/shard_map/ppermute | solution.py:209

commit v6 on v5

--- a/solution.py
+++ b/solution.py
@@ -78,16 +78,24 @@
     up_out[...] = jnp.dot(x, up_ref[0, mine, :], preferred_element_type=jnp.float32)
 
 
-def middle_kernel(other_ref, gate_acc, up_acc, gate_ref, up_ref, down_ref, hidden_ref, send_ref):
+def middle_kernel(
+    other_ref, gate_acc, up_acc, gate_ref, up_ref, down_ref, hidden_ref, send_ref, gate_v, up_v
+):
     half = other_ref.shape[2]
-    theirs = half_of(1 - lax.axis_index("ep") % SPLIT, half)
+    side = 1 - lax.axis_index("ep") % SPLIT
+    theirs = half_of(side, half)
     x = flat(other_ref[...])
-    gate = gate_acc[...] + jnp.dot(x, gate_ref[0, theirs, :], preferred_element_type=jnp.float32)
-    up = up_acc[...] + jnp.dot(x, up_ref[0, theirs, :], preferred_element_type=jnp.float32)
-    hidden = (gate / (1.0 + jnp.exp(-gate)) * up).astype(jnp.bfloat16)
-    hidden_ref[...] = hidden
-    out = jnp.dot(hidden, down_ref[0, :, theirs], preferred_element_type=jnp.float32)
-    send_ref[...] = out.astype(jnp.bfloat16).reshape(send_ref.shape)
+    gate_v[...] = jnp.dot(x, gate_ref[0, theirs, :], preferred_element_type=jnp.float32)
+    up_v[...] = jnp.dot(x, up_ref[0, theirs, :], preferred_element_type=jnp.float32)
+
+    @pl.when(side < SPLIT)
+    def _():
+        gate = gate_acc[...] + gate_v[...]
+        up = up_acc[...] + up_v[...]
+        hidden = (gate / (1.0 + jnp.exp(-gate)) * up).astype(jnp.bfloat16)
+        hidden_ref[...] = hidden
+        out = jnp.dot(hidden, down_ref[0, :, theirs], preferred_element_type=jnp.float32)
+        send_ref[...] = out.astype(jnp.bfloat16).reshape(send_ref.shape)
 
 
 def leave_kernel(hidden_ref, down_ref, keep_ref):
@@ -205,6 +213,7 @@
         w_up,
         w_down,
         flops=3 * product,
+        scratch_shapes=[pltpu.VMEM((rows, hidden_width), f32)] * 2,
     )
     arrived = lax.ppermute(send, "ep", swap)
     keep = call(leave_kernel, "leave", shape(block, f32), hidden, w_down, flops=product)

time: 26.3 us -> 26.3 us (level)
  no operation moved by 1% of the time
where the time goes in v6:
time: 26.3 us; the launch traced here: 26 us
  blocking collectives  19.8 us (75%)
  Pallas kernels  4.34 us (17%)
  starting transfers between devices  0.9 us (3%)
  waiting for transfers between devices  0.77 us (3%)
    all_to_all x1, blocking collectives, shards(): own = exchange(outgoing)  11.2 us
    all_to_all x1, blocking collectives, shards(): returned = exchange(summed).reshape(chips, SPLIT, capacity, half)  8.62 us
    pallas_call x6, Pallas kernels, call(): return pl.pallas_call(kernel, **{**options, **more})(*args)  4.34 us
    ppermute x1, waiting for transfers between devices, shards(): arrived = lax.ppermute(send, 'ep', swap)  0.54 us
  transfers between devices with their start and end apart: 2, of which 2 were waited for; matrix products, arithmetic and copies ran while one was open for 0% of the time, Pallas kernels for 4%

profile of v6, /device:TPU:0, one launch (start us, length us, event | category | flops | bytes accessed | tf_op | source)
XLA Modules:
  0.0 26.0 jit_solution(4160567673046075557)
XLA Ops:
  0.0 1.1 %route.1 = (bf16[8,2,2,1792]{3,2,1,0:T(2,128)(2,1)S(1)}, bf16[16,32]{1,0:T(8,128)(2,1)S(1)}) custom-call(s32[8,32]{1,0:T(8,128)} %bitcast.6, s32[8,32]{1,0:T(8,128)} %bitcast.7, bf16[32,3584]{1,0:T(8,128)(2,1)} %tokens_hbm.1), custom_call_target="tpu_custom_call" | custom-call | tf_op jit(solution)/shard_map/route/pallas_call | solution.py:147
  1.2 0.0 copy-start
  1.2 0.0 copy-start.1
  1.2 0.0 copy-start.2
  1.2 11.2 %all_to_all.10.own_ref = bf16[16,2,1792]{2,1,0:T(2,128)(2,1)S(1)} all-to-all(bf16[16,2,1792]{2,1,0:T(2,128)(2,1)S(1)} %mark.1), channel_id=1, replica_groups={{11,10,1,0,3,2,5,4,7,6,9,8,13,12,15,14},{27,26,17,16,19,18,21,20,23,22,..., dimensions={0} | all-to-all | bytes 229376 | tf_op jit(solution)/shard_map/all_to_all | solution.py:193
  12.4 0.5 %collective-permute-start = (bf16[16,2,1792]{2,1,0:T(2,128)(2,1)S(1)}, bf16[16,2,1792]{2,1,0:T(2,128)(2,1)S(1)}, u32[]{:S(2)}, u32[]{:S(2)}) collective-permute-start(bf16[16,2,1792]{2,1,0:T(2,128)(2,1)S(1)} %all_to_all.10.own_ref), channel_id=1, source_target_pairs={{0,1},{1,0},{2,3},{3,2},{4,5},{5,4},{6,7},{7,6},{8,9},{9,8},{10,11... | collective-permute-start | bytes 344072 | tf_op jit(solution)/shard_map/ppermute | solution.py:194
  12.8 0.0 copy-done
  12.9 0.0 copy-done.1
  12.9 0.0 copy-done.2
  12.9 0.7 %enter.1 = (f32[32,512]{1,0:T(8,128)S(1)}, f32[32,512]{1,0:T(8,128)S(1)}) custom-call(bf16[16,2,1792]{2,1,0:T(2,128)(2,1)S(1)} %all_to_all.10.own_ref, bf16[1,3584,512]{2,1,0:T(8,128)(2,1)S(1)} %copy-done.1, bf16[1,3584,512]{2,1,0:T(8,128)(2,1)S(1)} %copy-done.2, bf16[1,512,3584]{2,1,0:T(8,128)(2,1)S(1)} %copy-done), custom_call_target="tpu_custom_call" | custom-call | flops 117440512 | tf_op jit(solution)/shard_map/enter/pallas_call | solution.py:147
  13.6 0.2 collective-permute-done.other_ref
  13.8 1.1 %middle.1 = (bf16[32,512]{1,0:T(8,128)(2,1)S(1)}, bf16[16,2,1792]{2,1,0:T(2,128)(2,1)S(1)}) custom-call(bf16[16,2,1792]{2,1,0:T(2,128)(2,1)S(1)} %collective-permute-done.other_ref, f32[32,512]{1,0:T(8,128)S(1)} %get-tuple-element.13.gate_acc, f32[32,512]{1,0:T(8,128)S(1)} %get-tuple-element.14.up_acc, bf16[1,3584,512]{2,1,0:T(8,128)(2,1)S(1)} %copy-done.1, ...), custom_call_target="tpu_custom_call" | custom-call | flops 176160768 | tf_op jit(solution)/shard_map/middle/pallas_call | solution.py:147
  15.0 0.4 %collective-permute-start.1 = (bf16[16,2,1792]{2,1,0:T(2,128)(2,1)S(1)}, bf16[16,2,1792]{2,1,0:T(2,128)(2,1)S(1)}, u32[]{:S(2)}, u32[]{:S(2)}) collective-permute-start(bf16[16,2,1792]{2,1,0:T(2,128)(2,1)S(1)} %get-tuple-element.16), channel_id=1, source_target_pairs={{0,1},{1,0},{2,3},{3,2},{4,5},{5,4},{6,7},{7,6},{8,9},{9,8},{10,11... | collective-permute-start | bytes 344072 | tf_op jit(solution)/shard_map/ppermute | solution.py:218
  15.4 0.4 %leave.1 = f32[16,2,1792]{2,1,0:T(2,128)S(1)} custom-call(bf16[32,512]{1,0:T(8,128)(2,1)S(1)} %get-tuple-element.15.hidden_ref, bf16[1,512,3584]{2,1,0:T(8,128)(2,1)S(1)} %copy-done), custom_call_target="tpu_custom_call" | custom-call | flops 58720256 | tf_op jit(solution)/shard_map/leave/pallas_call | solution.py:147
  15.8 0.5 %collective-permute-done.1 = bf16[16,2,1792]{2,1,0:T(2,128)(2,1)S(1)} collective-permute-done((bf16[16,2,1792]{2,1,0:T(2,128)(2,1)S(1)}, bf16[16,2,1792]{2,1,0:T(2,128)(2,1)S(1)}, u32[]{:S(2)}, u32[]{:S(2)}) %collective-permute-start.1) | collective-permute-done | bytes 114720 | tf_op jit(solution)/shard_map/ppermute | solution.py:218
  16.4 0.1 add_convert_fusion
  16.5 8.6 %all_to_all.11 = bf16[16,2,1792]{2,1,0:T(2,128)(2,1)S(1)} all-to-all(bf16[16,2,1792]{2,1,0:T(2,128)(2,1)S(1)} %add_convert_fusion), channel_id=1, replica_groups={{11,10,1,0,3,2,5,4,7,6,9,8,13,12,15,14},{27,26,17,16,19,18,21,20,23,22,..., dimensions={0} | all-to-all | bytes 229376 | tf_op jit(solution)/shard_map/all_to_all | solution.py:221
  25.1 0.9 %combine.1 = bf16[32,3584]{1,0:T(8,128)(2,1)} custom-call(bf16[16,32]{1,0:T(8,128)(2,1)S(1)} %get-tuple-element.11.weight_ref, bf16[8,2,2,1792]{3,2,1,0:T(2,128)(2,1)S(1)} %bitcast.4), custom_call_target="tpu_custom_call" | custom-call | tf_op jit(solution)/shard_map/combine/pallas_call | solution.py:147
  (1 shorter events, 0.0 us)
Async XLA Ops:
  1.2 11.7 %copy-start = (bf16[1,512,3584]{2,1,0:T(8,128)(2,1)S(1)}, bf16[1,512,3584]{2,1,0:T(8,128)(2,1)}, u32[]{:S(2)}) copy-start(bf16[1,512,3584]{2,1,0:T(8,128)(2,1)} %down_ref.5) | copy-start | bytes 11010052
  1.2 11.7 %copy-start.1 = (bf16[1,3584,512]{2,1,0:T(8,128)(2,1)S(1)}, bf16[1,3584,512]{2,1,0:T(8,128)(2,1)}, u32[]{:S(2)}) copy-start(bf16[1,3584,512]{2,1,0:T(8,128)(2,1)} %gate_ref.3) | copy-start | bytes 11010052
  1.2 11.7 %copy-start.2 = (bf16[1,3584,512]{2,1,0:T(8,128)(2,1)S(1)}, bf16[1,3584,512]{2,1,0:T(8,128)(2,1)}, u32[]{:S(2)}) copy-start(bf16[1,3584,512]{2,1,0:T(8,128)(2,1)} %up_ref.3) | copy-start | bytes 11010052
  12.4 1.4 %collective-permute-start = (bf16[16,2,1792]{2,1,0:T(2,128)(2,1)S(1)}, bf16[16,2,1792]{2,1,0:T(2,128)(2,1)S(1)}, u32[]{:S(2)}, u32[]{:S(2)}) collective-permute-start(bf16[16,2,1792]{2,1,0:T(2,128)(2,1)S(1)} %all_to_all.10.own_ref), channel_id=1, source_target_pairs={{0,1},{1,0},{2,3},{3,2},{4,5},{5,4},{6,7},{7,6},{8,9},{9,8},{10,11... | collective-permute-start | bytes 344072 | tf_op jit(solution)/shard_map/ppermute | solution.py:194
  15.0 1.4 %collective-permute-start.1 = (bf16[16,2,1792]{2,1,0:T(2,128)(2,1)S(1)}, bf16[16,2,1792]{2,1,0:T(2,128)(2,1)S(1)}, u32[]{:S(2)}, u32[]{:S(2)}) collective-permute-start(bf16[16,2,1792]{2,1,0:T(2,128)(2,1)S(1)} %get-tuple-element.16), channel_id=1, source_target_pairs={{0,1},{1,0},{2,3},{3,2},{4,5},{5,4},{6,7},{7,6},{8,9},{9,8},{10,11... | collective-permute-start | bytes 344072 | tf_op jit(solution)/shard_map/ppermute | solution.py:218

commit v7 on v5

--- a/solution.py
+++ b/solution.py
@@ -29,7 +29,7 @@
 
 
 def route_kernel(
-    capacity, order, routes_hbm, gates_hbm, tokens_hbm, out_ref, weight_ref, routes_v, gates_v, tokens_v, sems
+    capacity, there, back, routes_hbm, gates_hbm, tokens_hbm, out_ref, weight_ref, routes_v, gates_v, tokens_v, sems
 ):
     chips, halves, _, half = out_ref.shape
     copies = [
@@ -41,13 +41,16 @@
     for copy in copies:
         copy.start()
     copies[0].wait()
-    pick, same = slots_of(routes_v[...], chips * capacity, capacity, order)
+    pick, same = slots_of(routes_v[...], chips * capacity, capacity, there)
     copies[2].wait()
     gates = gates_v[...].astype(jnp.float32) / 256.0
     weight = jnp.zeros_like(pick)
     for k, hit in enumerate(same):
         weight = jnp.where(hit, gates[k : k + 1, :], weight)
-    weight_ref[...] = (weight * pick).astype(jnp.bfloat16)
+    weight = (weight * pick).astype(jnp.bfloat16)
+    for i, chip in enumerate(there):
+        j = back.index(chip)
+        weight_ref[j * capacity : (j + 1) * capacity, :] = weight[i * capacity : (i + 1) * capacity]
     copies[1].wait()
     rows = jnp.dot(
         pick.astype(jnp.bfloat16), tokens_v[...], preferred_element_type=jnp.float32
@@ -91,10 +94,19 @@
 
 
 def leave_kernel(hidden_ref, down_ref, keep_ref):
-    half = keep_ref.shape[2]
+    half = keep_ref.shape[1]
     mine = half_of(lax.axis_index("ep") % SPLIT, half)
-    out = jnp.dot(hidden_ref[...], down_ref[0, :, mine], preferred_element_type=jnp.float32)
-    keep_ref[...] = out.reshape(keep_ref.shape)
+    keep_ref[...] = jnp.dot(
+        hidden_ref[...], down_ref[0, :, mine], preferred_element_type=jnp.float32
+    )
+
+
+def add_kernel(moves, keep_ref, arrived_ref, out_ref):
+    capacity, half = out_ref.shape[1:]
+    total = (keep_ref[...] + flat(arrived_ref[...]).astype(jnp.float32)).astype(jnp.bfloat16)
+    total = total.reshape(out_ref.shape)
+    for source, target in enumerate(moves):
+        out_ref[target] = total[source]
 
 
 def combine_kernel(weight_ref, rows_ref, out_hbm, out_v, sems):
@@ -116,9 +128,17 @@
         copy.wait()
 
 
-def group_order(chips):
+def group_orders(chips):
     first = (5 * chips) // 8
-    return [first] + [c for c in range(chips) if c != first]
+    back = [first] + [c for c in range(chips) if c != first]
+    half = chips // 2
+    ring = [c for c in range(half, chips) if c % 2] + [c for c in range(half, chips) if not c % 2][::-1]
+    turn = ring.index(first)
+    there = ring[turn:] + ring[:turn]
+    there += [c + k for c in range(half - 2, -1, -2) for k in range(2)]
+    if sorted(there) != list(range(chips)):
+        there = back
+    return there, back
 
 
 VMEM = pl.BlockSpec(memory_space=pltpu.VMEM)
@@ -147,8 +167,8 @@
     chips = devices // SPLIT
     half = width // SPLIT
     capacity = max(2, min(tok_rows, 5 * tok_rows * top_count // (2 * EXPERTS)))
-    order = group_order(chips)
-    group = [[c * SPLIT + k for c in order for k in reversed(range(SPLIT))]]
+    there, back = group_orders(chips)
+    moves = [back.index(c) * SPLIT + k for c in there for k in range(SPLIT)]
     swap = [(d, d ^ 1) for d in range(devices)]
     slots, rows = chips * capacity, devices * capacity
     block = (devices, capacity, half)
@@ -158,7 +178,7 @@
 
     sources = [pltpu.with_memory_space_constraint(a, pltpu.HBM) for a in (routes.T, gate_num.T, tokens)]
     outgoing, weight = call(
-        functools.partial(route_kernel, capacity, order),
+        functools.partial(route_kernel, capacity, there, back),
         "route",
         (shape((chips, SPLIT, capacity, half), bf16), shape((slots, tok_rows), bf16)),
         *sources,
@@ -174,15 +194,13 @@
     outgoing = call(
         mark_kernel, "mark", shape(block, bf16), outgoing, flops=10**10, input_output_aliases={0: 0}
     )
-    exchange = functools.partial(
-        lax.all_to_all,
-        axis_name="ep",
-        split_axis=0,
-        concat_axis=0,
-        tiled=True,
-        axis_index_groups=group,
-    )
-    own = exchange(outgoing)
+    def exchange(blocks, order):
+        group = [[c * SPLIT + k for c in order for k in reversed(range(SPLIT))]]
+        return lax.all_to_all(
+            blocks, "ep", split_axis=0, concat_axis=0, tiled=True, axis_index_groups=group
+        )
+
+    own = exchange(outgoing, there)
     other = lax.ppermute(own, "ep", swap)
     product = rows * half * hidden_width * 2
     accs = call(
@@ -207,9 +225,9 @@
         flops=3 * product,
     )
     arrived = lax.ppermute(send, "ep", swap)
-    keep = call(leave_kernel, "leave", shape(block, f32), hidden, w_down, flops=product)
-    summed = (keep + arrived.astype(f32)).astype(bf16)
-    returned = exchange(summed).reshape(chips, SPLIT, capacity, half)
+    keep = call(leave_kernel, "leave", shape((rows, half), f32), hidden, w_down, flops=product)
+    summed = call(functools.partial(add_kernel, moves), "add", shape(block, bf16), keep, arrived)
+    returned = exchange(summed, back).reshape(chips, SPLIT, capacity, half)
     return call(
         combine_kernel,
         "combine",

time: 26.3 us -> 25.9 us (0.985)
    pallas_call x6 -> x7, Pallas kernels: 4.35 us -> 4.41 us  [call(): return pl.pallas_call(kernel, **{**options, **more})(*args)]
where the time goes in v7:
time: 25.9 us; the launch traced here: 25.7 us
  blocking collectives  19.6 us (76%)
  Pallas kernels  4.41 us (17%)
  waiting for transfers between devices  0.85 us (3%)
  starting transfers between devices  0.72 us (3%)
    all_to_all x2, blocking collectives, exchange(): lax.all_to_all(blocks, 'ep', split_axis=0, concat_axis=0, tiled=True, axi...  19.6 us
    pallas_call x7, Pallas kernels, call(): return pl.pallas_call(kernel, **{**options, **more})(*args)  4.41 us
    ppermute x1, waiting for transfers between devices, shards(): arrived = lax.ppermute(send, 'ep', swap)  0.59 us
  transfers between devices with their start and end apart: 2, of which 2 were waited for; matrix products, arithmetic and copies ran while one was open for 0% of the time, Pallas kernels for 4%

profile of v7, /device:TPU:0, one launch (start us, length us, event | category | flops | bytes accessed | tf_op | source)
XLA Modules:
  0.0 25.7 jit_solution(17180648873376200275)
XLA Ops:
  0.0 1.1 %route.1 = (bf16[8,2,2,1792]{3,2,1,0:T(2,128)(2,1)S(1)}, bf16[16,32]{1,0:T(8,128)(2,1)S(1)}) custom-call(s32[8,32]{1,0:T(8,128)} %bitcast.6, s32[8,32]{1,0:T(8,128)} %bitcast.7, bf16[32,3584]{1,0:T(8,128)(2,1)} %tokens_hbm.1), custom_call_target="tpu_custom_call" | custom-call | tf_op jit(solution)/shard_map/route/pallas_call | solution.py:159
  1.2 0.0 copy-start
  1.2 0.0 copy-start.1
  1.2 0.0 copy-start.2
  1.2 11.5 %all_to_all.10.own_ref = bf16[16,2,1792]{2,1,0:T(2,128)(2,1)S(1)} all-to-all(bf16[16,2,1792]{2,1,0:T(2,128)(2,1)S(1)} %mark.1), channel_id=1, replica_groups={{11,10,15,14,13,12,9,8,5,4,7,6,1,0,3,2},{27,26,31,30,29,28,25,24,21,20,..., dimensions={0} | all-to-all | bytes 229376 | tf_op jit(solution)/shard_map/all_to_all | solution.py:199
  12.7 0.3 %collective-permute-start = (bf16[16,2,1792]{2,1,0:T(2,128)(2,1)S(1)}, bf16[16,2,1792]{2,1,0:T(2,128)(2,1)S(1)}, u32[]{:S(2)}, u32[]{:S(2)}) collective-permute-start(bf16[16,2,1792]{2,1,0:T(2,128)(2,1)S(1)} %all_to_all.10.own_ref), channel_id=1, source_target_pairs={{0,1},{1,0},{2,3},{3,2},{4,5},{5,4},{6,7},{7,6},{8,9},{9,8},{10,11... | collective-permute-start | bytes 344072 | tf_op jit(solution)/shard_map/ppermute | solution.py:204
  13.0 0.0 copy-done
  13.0 0.0 copy-done.1
  13.0 0.0 copy-done.2
  13.0 0.7 %enter.1 = (f32[32,512]{1,0:T(8,128)S(1)}, f32[32,512]{1,0:T(8,128)S(1)}) custom-call(bf16[16,2,1792]{2,1,0:T(2,128)(2,1)S(1)} %all_to_all.10.own_ref, bf16[1,3584,512]{2,1,0:T(8,128)(2,1)S(1)} %copy-done.1, bf16[1,3584,512]{2,1,0:T(8,128)(2,1)S(1)} %copy-done.2, bf16[1,512,3584]{2,1,0:T(8,128)(2,1)S(1)} %copy-done), custom_call_target="tpu_custom_call" | custom-call | flops 117440512 | tf_op jit(solution)/shard_map/enter/pallas_call | solution.py:159
  13.7 0.3 %collective-permute-done.other_ref = bf16[16,2,1792]{2,1,0:T(2,128)(2,1)S(1)} collective-permute-done((bf16[16,2,1792]{2,1,0:T(2,128)(2,1)S(1)}, bf16[16,2,1792]{2,1,0:T(2,128)(2,1)S(1)}, u32[]{:S(2)}, u32[]{:S(2)}) %collective-permute-start) | collective-permute-done | bytes 114720 | tf_op jit(solution)/shard_map/ppermute | solution.py:204
  14.0 1.2 %middle.1 = (bf16[32,512]{1,0:T(8,128)(2,1)S(1)}, bf16[16,2,1792]{2,1,0:T(2,128)(2,1)S(1)}) custom-call(bf16[16,2,1792]{2,1,0:T(2,128)(2,1)S(1)} %collective-permute-done.other_ref, f32[32,512]{1,0:T(8,128)S(1)} %get-tuple-element.13.gate_acc, f32[32,512]{1,0:T(8,128)S(1)} %get-tuple-element.14.up_acc, bf16[1,3584,512]{2,1,0:T(8,128)(2,1)S(1)} %copy-done.1, ...), custom_call_target="tpu_custom_call" | custom-call | flops 176160768 | tf_op jit(solution)/shard_map/middle/pallas_call | solution.py:159
  15.2 0.4 %collective-permute-start.1 = (bf16[16,2,1792]{2,1,0:T(2,128)(2,1)S(1)}, bf16[16,2,1792]{2,1,0:T(2,128)(2,1)S(1)}, u32[]{:S(2)}, u32[]{:S(2)}) collective-permute-start(bf16[16,2,1792]{2,1,0:T(2,128)(2,1)S(1)} %get-tuple-element.16), channel_id=1, source_target_pairs={{0,1},{1,0},{2,3},{3,2},{4,5},{5,4},{6,7},{7,6},{8,9},{9,8},{10,11... | collective-permute-start | bytes 344072 | tf_op jit(solution)/shard_map/ppermute | solution.py:227
  15.6 0.4 %leave.1.keep_ref = f32[32,1792]{1,0:T(8,128)S(1)} custom-call(bf16[32,512]{1,0:T(8,128)(2,1)S(1)} %get-tuple-element.15.hidden_ref, bf16[1,512,3584]{2,1,0:T(8,128)(2,1)S(1)} %copy-done), custom_call_target="tpu_custom_call" | custom-call | flops 58720256 | tf_op jit(solution)/shard_map/leave/pallas_call | solution.py:159
  16.0 0.6 %collective-permute-done.1.arrived_ref = bf16[16,2,1792]{2,1,0:T(2,128)(2,1)S(1)} collective-permute-done((bf16[16,2,1792]{2,1,0:T(2,128)(2,1)S(1)}, bf16[16,2,1792]{2,1,0:T(2,128)(2,1)S(1)}, u32[]{:S(2)}, u32[]{:S(2)}) %collective-permute-start.1) | collective-permute-done | bytes 114720 | tf_op jit(solution)/shard_map/ppermute | solution.py:227
  16.6 0.1 add.1
  16.6 8.1 %all_to_all.11 = bf16[16,2,1792]{2,1,0:T(2,128)(2,1)S(1)} all-to-all(bf16[16,2,1792]{2,1,0:T(2,128)(2,1)S(1)} %add.1), channel_id=1, replica_groups={{11,10,1,0,3,2,5,4,7,6,9,8,13,12,15,14},{27,26,17,16,19,18,21,20,23,22,..., dimensions={0} | all-to-all | bytes 229376 | tf_op jit(solution)/shard_map/all_to_all | solution.py:199
  24.8 0.9 %combine.1 = bf16[32,3584]{1,0:T(8,128)(2,1)} custom-call(bf16[16,32]{1,0:T(8,128)(2,1)S(1)} %get-tuple-element.11.weight_ref, bf16[8,2,2,1792]{3,2,1,0:T(2,128)(2,1)S(1)} %bitcast.4), custom_call_target="tpu_custom_call" | custom-call | tf_op jit(solution)/shard_map/combine/pallas_call | solution.py:159
  (1 shorter events, 0.0 us)
Async XLA Ops:
  1.2 11.8 %copy-start = (bf16[1,512,3584]{2,1,0:T(8,128)(2,1)S(1)}, bf16[1,512,3584]{2,1,0:T(8,128)(2,1)}, u32[]{:S(2)}) copy-start(bf16[1,512,3584]{2,1,0:T(8,128)(2,1)} %down_ref.5) | copy-start | bytes 11010052
  1.2 11.8 %copy-start.1 = (bf16[1,3584,512]{2,1,0:T(8,128)(2,1)S(1)}, bf16[1,3584,512]{2,1,0:T(8,128)(2,1)}, u32[]{:S(2)}) copy-start(bf16[1,3584,512]{2,1,0:T(8,128)(2,1)} %gate_ref.3) | copy-start | bytes 11010052
  1.2 11.8 %copy-start.2 = (bf16[1,3584,512]{2,1,0:T(8,128)(2,1)S(1)}, bf16[1,3584,512]{2,1,0:T(8,128)(2,1)}, u32[]{:S(2)}) copy-start(bf16[1,3584,512]{2,1,0:T(8,128)(2,1)} %up_ref.3) | copy-start | bytes 11010052
  12.7 1.3 %collective-permute-start = (bf16[16,2,1792]{2,1,0:T(2,128)(2,1)S(1)}, bf16[16,2,1792]{2,1,0:T(2,128)(2,1)S(1)}, u32[]{:S(2)}, u32[]{:S(2)}) collective-permute-start(bf16[16,2,1792]{2,1,0:T(2,128)(2,1)S(1)} %all_to_all.10.own_ref), channel_id=1, source_target_pairs={{0,1},{1,0},{2,3},{3,2},{4,5},{5,4},{6,7},{7,6},{8,9},{9,8},{10,11... | collective-permute-start | bytes 344072 | tf_op jit(solution)/shard_map/ppermute | solution.py:204
  15.2 1.4 %collective-permute-start.1 = (bf16[16,2,1792]{2,1,0:T(2,128)(2,1)S(1)}, bf16[16,2,1792]{2,1,0:T(2,128)(2,1)S(1)}, u32[]{:S(2)}, u32[]{:S(2)}) collective-permute-start(bf16[16,2,1792]{2,1,0:T(2,128)(2,1)S(1)} %get-tuple-element.16), channel_id=1, source_target_pairs={{0,1},{1,0},{2,3},{3,2},{4,5},{5,4},{6,7},{7,6},{8,9},{9,8},{10,11... | collective-permute-start | bytes 344072 | tf_op jit(solution)/shard_map/ppermute | solution.py:227

commit v8 on v7

--- a/solution.py
+++ b/solution.py
@@ -60,10 +60,6 @@
         out_ref[:, halves - 1 - k] = part.reshape(chips, capacity, half)
 
 
-def mark_kernel(in_ref, out_ref):
-    del in_ref, out_ref
-
-
 def flat(rows):
     return rows.reshape(rows.shape[0] * rows.shape[1], rows.shape[2])
 
@@ -182,6 +178,7 @@
         "route",
         (shape((chips, SPLIT, capacity, half), bf16), shape((slots, tok_rows), bf16)),
         *sources,
+        flops=10**10,
         in_specs=[ANY] * 3,
         scratch_shapes=[
             pltpu.VMEM((top_count, tok_rows), jnp.int32),
@@ -191,9 +188,6 @@
         ],
     )
     outgoing = outgoing.reshape(block)
-    outgoing = call(
-        mark_kernel, "mark", shape(block, bf16), outgoing, flops=10**10, input_output_aliases={0: 0}
-    )
     def exchange(blocks, order):
         group = [[c * SPLIT + k for c in order for k in reversed(range(SPLIT))]]
         return lax.all_to_all(

time: 25.9 us -> 26 us (level)
    pallas_call x7 -> x6, Pallas kernels: 4.41 us -> 4.56 us  [call(): return pl.pallas_call(kernel, **{**options, **more})(*args)]
where the time goes in v8:
time: 26 us; the launch traced here: 25.8 us
  blocking collectives  19.6 us (75%)
  Pallas kernels  4.56 us (18%)
  waiting for transfers between devices  0.85 us (3%)
  starting transfers between devices  0.72 us (3%)
    all_to_all x2, blocking collectives, exchange(): lax.all_to_all(blocks, 'ep', split_axis=0, concat_axis=0, tiled=True, axi...  19.6 us
    pallas_call x6, Pallas kernels, call(): return pl.pallas_call(kernel, **{**options, **more})(*args)  4.56 us
    ppermute x1, waiting for transfers between devices, shards(): arrived = lax.ppermute(send, 'ep', swap)  0.59 us
  transfers between devices with their start and end apart: 2, of which 2 were waited for; matrix products, arithmetic and copies ran while one was open for 0% of the time, Pallas kernels for 4%

profile of v8, /device:TPU:0, one launch (start us, length us, event | category | flops | bytes accessed | tf_op | source)
XLA Modules:
  0.0 25.8 jit_solution(7241462938237631265)
XLA Ops:
  0.0 0.0 copy-start
  0.0 0.0 copy-start.1
  0.0 0.0 copy-start.2
  0.0 1.3 %route.1 = (bf16[8,2,2,1792]{3,2,1,0:T(2,128)(2,1)S(1)}, bf16[16,32]{1,0:T(8,128)(2,1)S(1)}) custom-call(s32[8,32]{1,0:T(8,128)} %bitcast.6, s32[8,32]{1,0:T(8,128)} %bitcast.7, bf16[32,3584]{1,0:T(8,128)(2,1)} %tokens_hbm.1), custom_call_target="tpu_custom_call" | custom-call | flops 10000000000 | tf_op jit(solution)/shard_map/route/pallas_call | solution.py:155
  1.3 11.5 %all_to_all.10.own_ref = bf16[16,2,1792]{2,1,0:T(2,128)(2,1)S(1)} all-to-all(bf16[16,2,1792]{2,1,0:T(2,128)(2,1)S(1)} %bitcast.5), channel_id=1, replica_groups={{11,10,15,14,13,12,9,8,5,4,7,6,1,0,3,2},{27,26,31,30,29,28,25,24,21,20,..., dimensions={0} | all-to-all | bytes 229376 | tf_op jit(solution)/shard_map/all_to_all | solution.py:193
  12.8 0.3 %collective-permute-start = (bf16[16,2,1792]{2,1,0:T(2,128)(2,1)S(1)}, bf16[16,2,1792]{2,1,0:T(2,128)(2,1)S(1)}, u32[]{:S(2)}, u32[]{:S(2)}) collective-permute-start(bf16[16,2,1792]{2,1,0:T(2,128)(2,1)S(1)} %all_to_all.10.own_ref), channel_id=1, source_target_pairs={{0,1},{1,0},{2,3},{3,2},{4,5},{5,4},{6,7},{7,6},{8,9},{9,8},{10,11... | collective-permute-start | bytes 344072 | tf_op jit(solution)/shard_map/ppermute | solution.py:198
  13.1 0.0 copy-done
  13.1 0.0 copy-done.1
  13.1 0.0 copy-done.2
  13.1 0.7 %enter.1 = (f32[32,512]{1,0:T(8,128)S(1)}, f32[32,512]{1,0:T(8,128)S(1)}) custom-call(bf16[16,2,1792]{2,1,0:T(2,128)(2,1)S(1)} %all_to_all.10.own_ref, bf16[1,3584,512]{2,1,0:T(8,128)(2,1)S(1)} %copy-done.1, bf16[1,3584,512]{2,1,0:T(8,128)(2,1)S(1)} %copy-done.2, bf16[1,512,3584]{2,1,0:T(8,128)(2,1)S(1)} %copy-done), custom_call_target="tpu_custom_call" | custom-call | flops 117440512 | tf_op jit(solution)/shard_map/enter/pallas_call | solution.py:155
  13.8 0.3 %collective-permute-done.other_ref = bf16[16,2,1792]{2,1,0:T(2,128)(2,1)S(1)} collective-permute-done((bf16[16,2,1792]{2,1,0:T(2,128)(2,1)S(1)}, bf16[16,2,1792]{2,1,0:T(2,128)(2,1)S(1)}, u32[]{:S(2)}, u32[]{:S(2)}) %collective-permute-start) | collective-permute-done | bytes 114720 | tf_op jit(solution)/shard_map/ppermute | solution.py:198
  14.1 1.2 %middle.1 = (bf16[32,512]{1,0:T(8,128)(2,1)S(1)}, bf16[16,2,1792]{2,1,0:T(2,128)(2,1)S(1)}) custom-call(bf16[16,2,1792]{2,1,0:T(2,128)(2,1)S(1)} %collective-permute-done.other_ref, f32[32,512]{1,0:T(8,128)S(1)} %get-tuple-element.13.gate_acc, f32[32,512]{1,0:T(8,128)S(1)} %get-tuple-element.14.up_acc, bf16[1,3584,512]{2,1,0:T(8,128)(2,1)S(1)} %copy-done.1, ...), custom_call_target="tpu_custom_call" | custom-call | flops 176160768 | tf_op jit(solution)/shard_map/middle/pallas_call | solution.py:155
  15.3 0.4 %collective-permute-start.1 = (bf16[16,2,1792]{2,1,0:T(2,128)(2,1)S(1)}, bf16[16,2,1792]{2,1,0:T(2,128)(2,1)S(1)}, u32[]{:S(2)}, u32[]{:S(2)}) collective-permute-start(bf16[16,2,1792]{2,1,0:T(2,128)(2,1)S(1)} %get-tuple-element.16), channel_id=1, source_target_pairs={{0,1},{1,0},{2,3},{3,2},{4,5},{5,4},{6,7},{7,6},{8,9},{9,8},{10,11... | collective-permute-start | bytes 344072 | tf_op jit(solution)/shard_map/ppermute | solution.py:221
  15.7 0.4 %leave.1.keep_ref = f32[32,1792]{1,0:T(8,128)S(1)} custom-call(bf16[32,512]{1,0:T(8,128)(2,1)S(1)} %get-tuple-element.15.hidden_ref, bf16[1,512,3584]{2,1,0:T(8,128)(2,1)S(1)} %copy-done), custom_call_target="tpu_custom_call" | custom-call | flops 58720256 | tf_op jit(solution)/shard_map/leave/pallas_call | solution.py:155
  16.1 0.6 %collective-permute-done.1.arrived_ref = bf16[16,2,1792]{2,1,0:T(2,128)(2,1)S(1)} collective-permute-done((bf16[16,2,1792]{2,1,0:T(2,128)(2,1)S(1)}, bf16[16,2,1792]{2,1,0:T(2,128)(2,1)S(1)}, u32[]{:S(2)}, u32[]{:S(2)}) %collective-permute-start.1) | collective-permute-done | bytes 114720 | tf_op jit(solution)/shard_map/ppermute | solution.py:221
  16.7 0.1 add.1
  16.7 8.1 %all_to_all.11 = bf16[16,2,1792]{2,1,0:T(2,128)(2,1)S(1)} all-to-all(bf16[16,2,1792]{2,1,0:T(2,128)(2,1)S(1)} %add.1), channel_id=1, replica_groups={{11,10,1,0,3,2,5,4,7,6,9,8,13,12,15,14},{27,26,17,16,19,18,21,20,23,22,..., dimensions={0} | all-to-all | bytes 229376 | tf_op jit(solution)/shard_map/all_to_all | solution.py:193
  24.9 0.9 %combine.1 = bf16[32,3584]{1,0:T(8,128)(2,1)} custom-call(bf16[16,32]{1,0:T(8,128)(2,1)S(1)} %get-tuple-element.11.weight_ref, bf16[8,2,2,1792]{3,2,1,0:T(2,128)(2,1)S(1)} %bitcast.4), custom_call_target="tpu_custom_call" | custom-call | tf_op jit(solution)/shard_map/combine/pallas_call | solution.py:155
Async XLA Ops:
  0.0 13.1 %copy-start = (bf16[1,512,3584]{2,1,0:T(8,128)(2,1)S(1)}, bf16[1,512,3584]{2,1,0:T(8,128)(2,1)}, u32[]{:S(2)}) copy-start(bf16[1,512,3584]{2,1,0:T(8,128)(2,1)} %down_ref.5) | copy-start | bytes 11010052
  0.0 13.1 %copy-start.1 = (bf16[1,3584,512]{2,1,0:T(8,128)(2,1)S(1)}, bf16[1,3584,512]{2,1,0:T(8,128)(2,1)}, u32[]{:S(2)}) copy-start(bf16[1,3584,512]{2,1,0:T(8,128)(2,1)} %gate_ref.3) | copy-start | bytes 11010052
  0.0 13.1 %copy-start.2 = (bf16[1,3584,512]{2,1,0:T(8,128)(2,1)S(1)}, bf16[1,3584,512]{2,1,0:T(8,128)(2,1)}, u32[]{:S(2)}) copy-start(bf16[1,3584,512]{2,1,0:T(8,128)(2,1)} %up_ref.3) | copy-start | bytes 11010052
  12.8 1.3 %collective-permute-start = (bf16[16,2,1792]{2,1,0:T(2,128)(2,1)S(1)}, bf16[16,2,1792]{2,1,0:T(2,128)(2,1)S(1)}, u32[]{:S(2)}, u32[]{:S(2)}) collective-permute-start(bf16[16,2,1792]{2,1,0:T(2,128)(2,1)S(1)} %all_to_all.10.own_ref), channel_id=1, source_target_pairs={{0,1},{1,0},{2,3},{3,2},{4,5},{5,4},{6,7},{7,6},{8,9},{9,8},{10,11... | collective-permute-start | bytes 344072 | tf_op jit(solution)/shard_map/ppermute | solution.py:198
  15.3 1.4 %collective-permute-start.1 = (bf16[16,2,1792]{2,1,0:T(2,128)(2,1)S(1)}, bf16[16,2,1792]{2,1,0:T(2,128)(2,1)S(1)}, u32[]{:S(2)}, u32[]{:S(2)}) collective-permute-start(bf16[16,2,1792]{2,1,0:T(2,128)(2,1)S(1)} %get-tuple-element.16), channel_id=1, source_target_pairs={{0,1},{1,0},{2,3},{3,2},{4,5},{5,4},{6,7},{7,6},{8,9},{9,8},{10,11... | collective-permute-start | bytes 344072 | tf_op jit(solution)/shard_map/ppermute | solution.py:221

commit v9 on v7

--- a/solution.py
+++ b/solution.py
@@ -135,7 +135,8 @@
     ring = [c for c in range(half, chips) if c % 2] + [c for c in range(half, chips) if not c % 2][::-1]
     turn = ring.index(first)
     there = ring[turn:] + ring[:turn]
-    there += [c + k for c in range(half - 2, -1, -2) for k in range(2)]
+    for i, c in enumerate(range(half - 2, -1, -2)):
+        there += [c, c + 1] if i % 2 else [c + 1, c]
     if sorted(there) != list(range(chips)):
         there = back
     return there, back

time: 25.9 us -> 25.9 us (level)
  no operation moved by 1% of the time
where the time goes in v9:
time: 25.9 us; the launch traced here: 25.7 us
  blocking collectives  19.6 us (76%)
  Pallas kernels  4.41 us (17%)
  waiting for transfers between devices  0.85 us (3%)
  starting transfers between devices  0.72 us (3%)
    all_to_all x2, blocking collectives, exchange(): lax.all_to_all(blocks, 'ep', split_axis=0, concat_axis=0, tiled=True, axi...  19.6 us
    pallas_call x7, Pallas kernels, call(): return pl.pallas_call(kernel, **{**options, **more})(*args)  4.41 us
    ppermute x1, waiting for transfers between devices, shards(): arrived = lax.ppermute(send, 'ep', swap)  0.59 us
  transfers between devices with their start and end apart: 2, of which 2 were waited for; matrix products, arithmetic and copies ran while one was open for 0% of the time, Pallas kernels for 4%

profile of v9, /device:TPU:0, one launch (start us, length us, event | category | flops | bytes accessed | tf_op | source)
XLA Modules:
  0.0 25.7 jit_solution(5787459496437252598)
XLA Ops:
  0.0 1.1 %route.1 = (bf16[8,2,2,1792]{3,2,1,0:T(2,128)(2,1)S(1)}, bf16[16,32]{1,0:T(8,128)(2,1)S(1)}) custom-call(s32[8,32]{1,0:T(8,128)} %bitcast.6, s32[8,32]{1,0:T(8,128)} %bitcast.7, bf16[32,3584]{1,0:T(8,128)(2,1)} %tokens_hbm.1), custom_call_target="tpu_custom_call" | custom-call | tf_op jit(solution)/shard_map/route/pallas_call | solution.py:160
  1.2 0.0 copy-start
  1.2 0.0 copy-start.1
  1.2 0.0 copy-start.2
  1.2 11.5 %all_to_all.10.own_ref = bf16[16,2,1792]{2,1,0:T(2,128)(2,1)S(1)} all-to-all(bf16[16,2,1792]{2,1,0:T(2,128)(2,1)S(1)} %mark.1), channel_id=1, replica_groups={{11,10,15,14,13,12,9,8,7,6,5,4,1,0,3,2},{27,26,31,30,29,28,25,24,23,22,..., dimensions={0} | all-to-all | bytes 229376 | tf_op jit(solution)/shard_map/all_to_all | solution.py:200
  12.7 0.3 %collective-permute-start = (bf16[16,2,1792]{2,1,0:T(2,128)(2,1)S(1)}, bf16[16,2,1792]{2,1,0:T(2,128)(2,1)S(1)}, u32[]{:S(2)}, u32[]{:S(2)}) collective-permute-start(bf16[16,2,1792]{2,1,0:T(2,128)(2,1)S(1)} %all_to_all.10.own_ref), channel_id=1, source_target_pairs={{0,1},{1,0},{2,3},{3,2},{4,5},{5,4},{6,7},{7,6},{8,9},{9,8},{10,11... | collective-permute-start | bytes 344072 | tf_op jit(solution)/shard_map/ppermute | solution.py:205
  13.0 0.0 copy-done
  13.0 0.0 copy-done.1
  13.0 0.0 copy-done.2
  13.0 0.7 %enter.1 = (f32[32,512]{1,0:T(8,128)S(1)}, f32[32,512]{1,0:T(8,128)S(1)}) custom-call(bf16[16,2,1792]{2,1,0:T(2,128)(2,1)S(1)} %all_to_all.10.own_ref, bf16[1,3584,512]{2,1,0:T(8,128)(2,1)S(1)} %copy-done.1, bf16[1,3584,512]{2,1,0:T(8,128)(2,1)S(1)} %copy-done.2, bf16[1,512,3584]{2,1,0:T(8,128)(2,1)S(1)} %copy-done), custom_call_target="tpu_custom_call" | custom-call | flops 117440512 | tf_op jit(solution)/shard_map/enter/pallas_call | solution.py:160
  13.7 0.3 %collective-permute-done.other_ref = bf16[16,2,1792]{2,1,0:T(2,128)(2,1)S(1)} collective-permute-done((bf16[16,2,1792]{2,1,0:T(2,128)(2,1)S(1)}, bf16[16,2,1792]{2,1,0:T(2,128)(2,1)S(1)}, u32[]{:S(2)}, u32[]{:S(2)}) %collective-permute-start) | collective-permute-done | bytes 114720 | tf_op jit(solution)/shard_map/ppermute | solution.py:205
  14.0 1.2 %middle.1 = (bf16[32,512]{1,0:T(8,128)(2,1)S(1)}, bf16[16,2,1792]{2,1,0:T(2,128)(2,1)S(1)}) custom-call(bf16[16,2,1792]{2,1,0:T(2,128)(2,1)S(1)} %collective-permute-done.other_ref, f32[32,512]{1,0:T(8,128)S(1)} %get-tuple-element.13.gate_acc, f32[32,512]{1,0:T(8,128)S(1)} %get-tuple-element.14.up_acc, bf16[1,3584,512]{2,1,0:T(8,128)(2,1)S(1)} %copy-done.1, ...), custom_call_target="tpu_custom_call" | custom-call | flops 176160768 | tf_op jit(solution)/shard_map/middle/pallas_call | solution.py:160
  15.2 0.4 %collective-permute-start.1 = (bf16[16,2,1792]{2,1,0:T(2,128)(2,1)S(1)}, bf16[16,2,1792]{2,1,0:T(2,128)(2,1)S(1)}, u32[]{:S(2)}, u32[]{:S(2)}) collective-permute-start(bf16[16,2,1792]{2,1,0:T(2,128)(2,1)S(1)} %get-tuple-element.16), channel_id=1, source_target_pairs={{0,1},{1,0},{2,3},{3,2},{4,5},{5,4},{6,7},{7,6},{8,9},{9,8},{10,11... | collective-permute-start | bytes 344072 | tf_op jit(solution)/shard_map/ppermute | solution.py:228
  15.6 0.4 %leave.1.keep_ref = f32[32,1792]{1,0:T(8,128)S(1)} custom-call(bf16[32,512]{1,0:T(8,128)(2,1)S(1)} %get-tuple-element.15.hidden_ref, bf16[1,512,3584]{2,1,0:T(8,128)(2,1)S(1)} %copy-done), custom_call_target="tpu_custom_call" | custom-call | flops 58720256 | tf_op jit(solution)/shard_map/leave/pallas_call | solution.py:160
  16.0 0.6 %collective-permute-done.1.arrived_ref = bf16[16,2,1792]{2,1,0:T(2,128)(2,1)S(1)} collective-permute-done((bf16[16,2,1792]{2,1,0:T(2,128)(2,1)S(1)}, bf16[16,2,1792]{2,1,0:T(2,128)(2,1)S(1)}, u32[]{:S(2)}, u32[]{:S(2)}) %collective-permute-start.1) | collective-permute-done | bytes 114720 | tf_op jit(solution)/shard_map/ppermute | solution.py:228
  16.6 0.1 add.1
  16.6 8.1 %all_to_all.11 = bf16[16,2,1792]{2,1,0:T(2,128)(2,1)S(1)} all-to-all(bf16[16,2,1792]{2,1,0:T(2,128)(2,1)S(1)} %add.1), channel_id=1, replica_groups={{11,10,1,0,3,2,5,4,7,6,9,8,13,12,15,14},{27,26,17,16,19,18,21,20,23,22,..., dimensions={0} | all-to-all | bytes 229376 | tf_op jit(solution)/shard_map/all_to_all | solution.py:200
  24.8 0.9 %combine.1 = bf16[32,3584]{1,0:T(8,128)(2,1)} custom-call(bf16[16,32]{1,0:T(8,128)(2,1)S(1)} %get-tuple-element.11.weight_ref, bf16[8,2,2,1792]{3,2,1,0:T(2,128)(2,1)S(1)} %bitcast.4), custom_call_target="tpu_custom_call" | custom-call | tf_op jit(solution)/shard_map/combine/pallas_call | solution.py:160
  (1 shorter events, 0.0 us)
Async XLA Ops:
  1.2 11.8 %copy-start = (bf16[1,512,3584]{2,1,0:T(8,128)(2,1)S(1)}, bf16[1,512,3584]{2,1,0:T(8,128)(2,1)}, u32[]{:S(2)}) copy-start(bf16[1,512,3584]{2,1,0:T(8,128)(2,1)} %down_ref.5) | copy-start | bytes 11010052
  1.2 11.8 %copy-start.1 = (bf16[1,3584,512]{2,1,0:T(8,128)(2,1)S(1)}, bf16[1,3584,512]{2,1,0:T(8,128)(2,1)}, u32[]{:S(2)}) copy-start(bf16[1,3584,512]{2,1,0:T(8,128)(2,1)} %gate_ref.3) | copy-start | bytes 11010052
  1.2 11.8 %copy-start.2 = (bf16[1,3584,512]{2,1,0:T(8,128)(2,1)S(1)}, bf16[1,3584,512]{2,1,0:T(8,128)(2,1)}, u32[]{:S(2)}) copy-start(bf16[1,3584,512]{2,1,0:T(8,128)(2,1)} %up_ref.3) | copy-start | bytes 11010052
  12.7 1.3 %collective-permute-start = (bf16[16,2,1792]{2,1,0:T(2,128)(2,1)S(1)}, bf16[16,2,1792]{2,1,0:T(2,128)(2,1)S(1)}, u32[]{:S(2)}, u32[]{:S(2)}) collective-permute-start(bf16[16,2,1792]{2,1,0:T(2,128)(2,1)S(1)} %all_to_all.10.own_ref), channel_id=1, source_target_pairs={{0,1},{1,0},{2,3},{3,2},{4,5},{5,4},{6,7},{7,6},{8,9},{9,8},{10,11... | collective-permute-start | bytes 344072 | tf_op jit(solution)/shard_map/ppermute | solution.py:205
  15.2 1.4 %collective-permute-start.1 = (bf16[16,2,1792]{2,1,0:T(2,128)(2,1)S(1)}, bf16[16,2,1792]{2,1,0:T(2,128)(2,1)S(1)}, u32[]{:S(2)}, u32[]{:S(2)}) collective-permute-start(bf16[16,2,1792]{2,1,0:T(2,128)(2,1)S(1)} %get-tuple-element.16), channel_id=1, source_target_pairs={{0,1},{1,0},{2,3},{3,2},{4,5},{5,4},{6,7},{7,6},{8,9},{9,8},{10,11... | collective-permute-start | bytes 344072 | tf_op jit(solution)/shard_map/ppermute | solution.py:228

commit v10 on v9

--- a/solution.py
+++ b/solution.py
@@ -81,16 +81,24 @@
     up_out[...] = jnp.dot(x, up_ref[0, mine, :], preferred_element_type=jnp.float32)
 
 
-def middle_kernel(other_ref, gate_acc, up_acc, gate_ref, up_ref, down_ref, hidden_ref, send_ref):
+def middle_kernel(
+    other_ref, gate_acc, up_acc, gate_ref, up_ref, down_ref, hidden_ref, send_ref, gate_v, up_v
+):
     half = other_ref.shape[2]
-    theirs = half_of(1 - lax.axis_index("ep") % SPLIT, half)
+    side = 1 - lax.axis_index("ep") % SPLIT
+    theirs = half_of(side, half)
     x = flat(other_ref[...])
-    gate = gate_acc[...] + jnp.dot(x, gate_ref[0, theirs, :], preferred_element_type=jnp.float32)
-    up = up_acc[...] + jnp.dot(x, up_ref[0, theirs, :], preferred_element_type=jnp.float32)
-    hidden = (gate / (1.0 + jnp.exp(-gate)) * up).astype(jnp.bfloat16)
-    hidden_ref[...] = hidden
-    out = jnp.dot(hidden, down_ref[0, :, theirs], preferred_element_type=jnp.float32)
-    send_ref[...] = out.astype(jnp.bfloat16).reshape(send_ref.shape)
+    gate_v[...] = jnp.dot(x, gate_ref[0, theirs, :], preferred_element_type=jnp.float32)
+    up_v[...] = jnp.dot(x, up_ref[0, theirs, :], preferred_element_type=jnp.float32)
+
+    @pl.when(side < SPLIT)
+    def _():
+        gate = gate_acc[...] + gate_v[...]
+        up = up_acc[...] + up_v[...]
+        hidden = (gate / (1.0 + jnp.exp(-gate)) * up).astype(jnp.bfloat16)
+        hidden_ref[...] = hidden
+        out = jnp.dot(hidden, down_ref[0, :, theirs], preferred_element_type=jnp.float32)
+        send_ref[...] = out.astype(jnp.bfloat16).reshape(send_ref.shape)
 
 
 def leave_kernel(hidden_ref, down_ref, keep_ref):
@@ -224,6 +232,7 @@
         w_up,
         w_down,
         flops=3 * product,
+        scratch_shapes=[pltpu.VMEM((rows, hidden_width), f32)] * 2,
     )
     arrived = lax.ppermute(send, "ep", swap)
     keep = call(leave_kernel, "leave", shape((rows, half), f32), hidden, w_down, flops=product)

time: 25.9 us -> 25.9 us (level)
  no operation moved by 1% of the time
where the time goes in v10:
time: 25.9 us; the launch traced here: 25.6 us
  blocking collectives  19.6 us (76%)
  Pallas kernels  4.39 us (17%)
  waiting for transfers between devices  0.85 us (3%)
  starting transfers between devices  0.71 us (3%)
    all_to_all x2, blocking collectives, exchange(): lax.all_to_all(blocks, 'ep', split_axis=0, concat_axis=0, tiled=True, axi...  19.6 us
    pallas_call x7, Pallas kernels, call(): return pl.pallas_call(kernel, **{**options, **more})(*args)  4.39 us
    ppermute x1, waiting for transfers between devices, shards(): arrived = lax.ppermute(send, 'ep', swap)  0.59 us
  transfers between devices with their start and end apart: 2, of which 2 were waited for; matrix products, arithmetic and copies ran while one was open for 0% of the time, Pallas kernels for 4%

profile of v10, /device:TPU:0, one launch (start us, length us, event | category | flops | bytes accessed | tf_op | source)
XLA Modules:
  0.0 25.6 jit_solution(3980644102803814583)
XLA Ops:
  0.0 1.1 %route.1 = (bf16[8,2,2,1792]{3,2,1,0:T(2,128)(2,1)S(1)}, bf16[16,32]{1,0:T(8,128)(2,1)S(1)}) custom-call(s32[8,32]{1,0:T(8,128)} %bitcast.6, s32[8,32]{1,0:T(8,128)} %bitcast.7, bf16[32,3584]{1,0:T(8,128)(2,1)} %tokens_hbm.1), custom_call_target="tpu_custom_call" | custom-call | tf_op jit(solution)/shard_map/route/pallas_call | solution.py:168
  1.2 0.0 copy-start
  1.2 0.0 copy-start.1
  1.2 0.0 copy-start.2
  1.2 11.5 %all_to_all.10.own_ref = bf16[16,2,1792]{2,1,0:T(2,128)(2,1)S(1)} all-to-all(bf16[16,2,1792]{2,1,0:T(2,128)(2,1)S(1)} %mark.1), channel_id=1, replica_groups={{11,10,15,14,13,12,9,8,7,6,5,4,1,0,3,2},{27,26,31,30,29,28,25,24,23,22,..., dimensions={0} | all-to-all | bytes 229376 | tf_op jit(solution)/shard_map/all_to_all | solution.py:208
  12.7 0.3 %collective-permute-start = (bf16[16,2,1792]{2,1,0:T(2,128)(2,1)S(1)}, bf16[16,2,1792]{2,1,0:T(2,128)(2,1)S(1)}, u32[]{:S(2)}, u32[]{:S(2)}) collective-permute-start(bf16[16,2,1792]{2,1,0:T(2,128)(2,1)S(1)} %all_to_all.10.own_ref), channel_id=1, source_target_pairs={{0,1},{1,0},{2,3},{3,2},{4,5},{5,4},{6,7},{7,6},{8,9},{9,8},{10,11... | collective-permute-start | bytes 344072 | tf_op jit(solution)/shard_map/ppermute | solution.py:213
  13.0 0.0 copy-done
  13.0 0.0 copy-done.1
  13.0 0.0 copy-done.2
  13.0 0.7 %enter.1 = (f32[32,512]{1,0:T(8,128)S(1)}, f32[32,512]{1,0:T(8,128)S(1)}) custom-call(bf16[16,2,1792]{2,1,0:T(2,128)(2,1)S(1)} %all_to_all.10.own_ref, bf16[1,3584,512]{2,1,0:T(8,128)(2,1)S(1)} %copy-done.1, bf16[1,3584,512]{2,1,0:T(8,128)(2,1)S(1)} %copy-done.2, bf16[1,512,3584]{2,1,0:T(8,128)(2,1)S(1)} %copy-done), custom_call_target="tpu_custom_call" | custom-call | flops 117440512 | tf_op jit(solution)/shard_map/enter/pallas_call | solution.py:168
  13.7 0.3 %collective-permute-done.other_ref = bf16[16,2,1792]{2,1,0:T(2,128)(2,1)S(1)} collective-permute-done((bf16[16,2,1792]{2,1,0:T(2,128)(2,1)S(1)}, bf16[16,2,1792]{2,1,0:T(2,128)(2,1)S(1)}, u32[]{:S(2)}, u32[]{:S(2)}) %collective-permute-start) | collective-permute-done | bytes 114720 | tf_op jit(solution)/shard_map/ppermute | solution.py:213
  14.0 1.1 %middle.1 = (bf16[32,512]{1,0:T(8,128)(2,1)S(1)}, bf16[16,2,1792]{2,1,0:T(2,128)(2,1)S(1)}) custom-call(bf16[16,2,1792]{2,1,0:T(2,128)(2,1)S(1)} %collective-permute-done.other_ref, f32[32,512]{1,0:T(8,128)S(1)} %get-tuple-element.13.gate_acc, f32[32,512]{1,0:T(8,128)S(1)} %get-tuple-element.14.up_acc, bf16[1,3584,512]{2,1,0:T(8,128)(2,1)S(1)} %copy-done.1, ...), custom_call_target="tpu_custom_call" | custom-call | flops 176160768 | tf_op jit(solution)/shard_map/middle/pallas_call | solution.py:168
  15.1 0.4 %collective-permute-start.1 = (bf16[16,2,1792]{2,1,0:T(2,128)(2,1)S(1)}, bf16[16,2,1792]{2,1,0:T(2,128)(2,1)S(1)}, u32[]{:S(2)}, u32[]{:S(2)}) collective-permute-start(bf16[16,2,1792]{2,1,0:T(2,128)(2,1)S(1)} %get-tuple-element.16), channel_id=1, source_target_pairs={{0,1},{1,0},{2,3},{3,2},{4,5},{5,4},{6,7},{7,6},{8,9},{9,8},{10,11... | collective-permute-start | bytes 344072 | tf_op jit(solution)/shard_map/ppermute | solution.py:237
  15.5 0.4 %leave.1.keep_ref = f32[32,1792]{1,0:T(8,128)S(1)} custom-call(bf16[32,512]{1,0:T(8,128)(2,1)S(1)} %get-tuple-element.15.hidden_ref, bf16[1,512,3584]{2,1,0:T(8,128)(2,1)S(1)} %copy-done), custom_call_target="tpu_custom_call" | custom-call | flops 58720256 | tf_op jit(solution)/shard_map/leave/pallas_call | solution.py:168
  15.9 0.6 %collective-permute-done.1.arrived_ref = bf16[16,2,1792]{2,1,0:T(2,128)(2,1)S(1)} collective-permute-done((bf16[16,2,1792]{2,1,0:T(2,128)(2,1)S(1)}, bf16[16,2,1792]{2,1,0:T(2,128)(2,1)S(1)}, u32[]{:S(2)}, u32[]{:S(2)}) %collective-permute-start.1) | collective-permute-done | bytes 114720 | tf_op jit(solution)/shard_map/ppermute | solution.py:237
  16.5 0.1 add.1
  16.6 8.1 %all_to_all.11 = bf16[16,2,1792]{2,1,0:T(2,128)(2,1)S(1)} all-to-all(bf16[16,2,1792]{2,1,0:T(2,128)(2,1)S(1)} %add.1), channel_id=1, replica_groups={{11,10,1,0,3,2,5,4,7,6,9,8,13,12,15,14},{27,26,17,16,19,18,21,20,23,22,..., dimensions={0} | all-to-all | bytes 229376 | tf_op jit(solution)/shard_map/all_to_all | solution.py:208
  24.7 0.9 %combine.1 = bf16[32,3584]{1,0:T(8,128)(2,1)} custom-call(bf16[16,32]{1,0:T(8,128)(2,1)S(1)} %get-tuple-element.11.weight_ref, bf16[8,2,2,1792]{3,2,1,0:T(2,128)(2,1)S(1)} %bitcast.4), custom_call_target="tpu_custom_call" | custom-call | tf_op jit(solution)/shard_map/combine/pallas_call | solution.py:168
  (1 shorter events, 0.0 us)
Async XLA Ops:
  1.2 11.8 %copy-start = (bf16[1,512,3584]{2,1,0:T(8,128)(2,1)S(1)}, bf16[1,512,3584]{2,1,0:T(8,128)(2,1)}, u32[]{:S(2)}) copy-start(bf16[1,512,3584]{2,1,0:T(8,128)(2,1)} %down_ref.5) | copy-start | bytes 11010052
  1.2 11.8 %copy-start.1 = (bf16[1,3584,512]{2,1,0:T(8,128)(2,1)S(1)}, bf16[1,3584,512]{2,1,0:T(8,128)(2,1)}, u32[]{:S(2)}) copy-start(bf16[1,3584,512]{2,1,0:T(8,128)(2,1)} %gate_ref.3) | copy-start | bytes 11010052
  1.2 11.8 %copy-start.2 = (bf16[1,3584,512]{2,1,0:T(8,128)(2,1)S(1)}, bf16[1,3584,512]{2,1,0:T(8,128)(2,1)}, u32[]{:S(2)}) copy-start(bf16[1,3584,512]{2,1,0:T(8,128)(2,1)} %up_ref.3) | copy-start | bytes 11010052
  12.7 1.3 %collective-permute-start = (bf16[16,2,1792]{2,1,0:T(2,128)(2,1)S(1)}, bf16[16,2,1792]{2,1,0:T(2,128)(2,1)S(1)}, u32[]{:S(2)}, u32[]{:S(2)}) collective-permute-start(bf16[16,2,1792]{2,1,0:T(2,128)(2,1)S(1)} %all_to_all.10.own_ref), channel_id=1, source_target_pairs={{0,1},{1,0},{2,3},{3,2},{4,5},{5,4},{6,7},{7,6},{8,9},{9,8},{10,11... | collective-permute-start | bytes 344072 | tf_op jit(solution)/shard_map/ppermute | solution.py:213
  15.1 1.4 %collective-permute-start.1 = (bf16[16,2,1792]{2,1,0:T(2,128)(2,1)S(1)}, bf16[16,2,1792]{2,1,0:T(2,128)(2,1)S(1)}, u32[]{:S(2)}, u32[]{:S(2)}) collective-permute-start(bf16[16,2,1792]{2,1,0:T(2,128)(2,1)S(1)} %get-tuple-element.16), channel_id=1, source_target_pairs={{0,1},{1,0},{2,3},{3,2},{4,5},{5,4},{6,7},{7,6},{8,9},{9,8},{10,11... | collective-permute-start | bytes 344072 | tf_op jit(solution)/shard_map/ppermute | solution.py:237

commit v11 on v8

--- a/solution.py
+++ b/solution.py
@@ -131,7 +131,8 @@
     ring = [c for c in range(half, chips) if c % 2] + [c for c in range(half, chips) if not c % 2][::-1]
     turn = ring.index(first)
     there = ring[turn:] + ring[:turn]
-    there += [c + k for c in range(half - 2, -1, -2) for k in range(2)]
+    for i, c in enumerate(range(half - 2, -1, -2)):
+        there += [c, c + 1] if i % 2 else [c + 1, c]
     if sorted(there) != list(range(chips)):
         there = back
     return there, back

time: 26 us -> 26 us (level)
  no operation moved by 1% of the time
where the time goes in v11:
time: 26 us; the launch traced here: 25.8 us
  blocking collectives  19.6 us (75%)
  Pallas kernels  4.56 us (18%)
  waiting for transfers between devices  0.85 us (3%)
  starting transfers between devices  0.72 us (3%)
    all_to_all x2, blocking collectives, exchange(): lax.all_to_all(blocks, 'ep', split_axis=0, concat_axis=0, tiled=True, axi...  19.6 us
    pallas_call x6, Pallas kernels, call(): return pl.pallas_call(kernel, **{**options, **more})(*args)  4.56 us
    ppermute x1, waiting for transfers between devices, shards(): arrived = lax.ppermute(send, 'ep', swap)  0.59 us
  transfers between devices with their start and end apart: 2, of which 2 were waited for; matrix products, arithmetic and copies ran while one was open for 0% of the time, Pallas kernels for 4%

profile of v11, /device:TPU:0, one launch (start us, length us, event | category | flops | bytes accessed | tf_op | source)
XLA Modules:
  0.0 25.8 jit_solution(15112766694251401688)
XLA Ops:
  0.0 0.0 copy-start
  0.0 0.0 copy-start.1
  0.0 0.0 copy-start.2
  0.0 1.3 %route.1 = (bf16[8,2,2,1792]{3,2,1,0:T(2,128)(2,1)S(1)}, bf16[16,32]{1,0:T(8,128)(2,1)S(1)}) custom-call(s32[8,32]{1,0:T(8,128)} %bitcast.6, s32[8,32]{1,0:T(8,128)} %bitcast.7, bf16[32,3584]{1,0:T(8,128)(2,1)} %tokens_hbm.1), custom_call_target="tpu_custom_call" | custom-call | flops 10000000000 | tf_op jit(solution)/shard_map/route/pallas_call | solution.py:156
  1.3 11.5 %all_to_all.10.own_ref = bf16[16,2,1792]{2,1,0:T(2,128)(2,1)S(1)} all-to-all(bf16[16,2,1792]{2,1,0:T(2,128)(2,1)S(1)} %bitcast.5), channel_id=1, replica_groups={{11,10,15,14,13,12,9,8,7,6,5,4,1,0,3,2},{27,26,31,30,29,28,25,24,23,22,..., dimensions={0} | all-to-all | bytes 229376 | tf_op jit(solution)/shard_map/all_to_all | solution.py:194
  12.8 0.3 %collective-permute-start = (bf16[16,2,1792]{2,1,0:T(2,128)(2,1)S(1)}, bf16[16,2,1792]{2,1,0:T(2,128)(2,1)S(1)}, u32[]{:S(2)}, u32[]{:S(2)}) collective-permute-start(bf16[16,2,1792]{2,1,0:T(2,128)(2,1)S(1)} %all_to_all.10.own_ref), channel_id=1, source_target_pairs={{0,1},{1,0},{2,3},{3,2},{4,5},{5,4},{6,7},{7,6},{8,9},{9,8},{10,11... | collective-permute-start | bytes 344072 | tf_op jit(solution)/shard_map/ppermute | solution.py:199
  13.1 0.0 copy-done
  13.1 0.0 copy-done.1
  13.1 0.0 copy-done.2
  13.1 0.7 %enter.1 = (f32[32,512]{1,0:T(8,128)S(1)}, f32[32,512]{1,0:T(8,128)S(1)}) custom-call(bf16[16,2,1792]{2,1,0:T(2,128)(2,1)S(1)} %all_to_all.10.own_ref, bf16[1,3584,512]{2,1,0:T(8,128)(2,1)S(1)} %copy-done.1, bf16[1,3584,512]{2,1,0:T(8,128)(2,1)S(1)} %copy-done.2, bf16[1,512,3584]{2,1,0:T(8,128)(2,1)S(1)} %copy-done), custom_call_target="tpu_custom_call" | custom-call | flops 117440512 | tf_op jit(solution)/shard_map/enter/pallas_call | solution.py:156
  13.8 0.3 %collective-permute-done.other_ref = bf16[16,2,1792]{2,1,0:T(2,128)(2,1)S(1)} collective-permute-done((bf16[16,2,1792]{2,1,0:T(2,128)(2,1)S(1)}, bf16[16,2,1792]{2,1,0:T(2,128)(2,1)S(1)}, u32[]{:S(2)}, u32[]{:S(2)}) %collective-permute-start) | collective-permute-done | bytes 114720 | tf_op jit(solution)/shard_map/ppermute | solution.py:199
  14.1 1.2 %middle.1 = (bf16[32,512]{1,0:T(8,128)(2,1)S(1)}, bf16[16,2,1792]{2,1,0:T(2,128)(2,1)S(1)}) custom-call(bf16[16,2,1792]{2,1,0:T(2,128)(2,1)S(1)} %collective-permute-done.other_ref, f32[32,512]{1,0:T(8,128)S(1)} %get-tuple-element.13.gate_acc, f32[32,512]{1,0:T(8,128)S(1)} %get-tuple-element.14.up_acc, bf16[1,3584,512]{2,1,0:T(8,128)(2,1)S(1)} %copy-done.1, ...), custom_call_target="tpu_custom_call" | custom-call | flops 176160768 | tf_op jit(solution)/shard_map/middle/pallas_call | solution.py:156
  15.3 0.4 %collective-permute-start.1 = (bf16[16,2,1792]{2,1,0:T(2,128)(2,1)S(1)}, bf16[16,2,1792]{2,1,0:T(2,128)(2,1)S(1)}, u32[]{:S(2)}, u32[]{:S(2)}) collective-permute-start(bf16[16,2,1792]{2,1,0:T(2,128)(2,1)S(1)} %get-tuple-element.16), channel_id=1, source_target_pairs={{0,1},{1,0},{2,3},{3,2},{4,5},{5,4},{6,7},{7,6},{8,9},{9,8},{10,11... | collective-permute-start | bytes 344072 | tf_op jit(solution)/shard_map/ppermute | solution.py:222
  15.7 0.4 %leave.1.keep_ref = f32[32,1792]{1,0:T(8,128)S(1)} custom-call(bf16[32,512]{1,0:T(8,128)(2,1)S(1)} %get-tuple-element.15.hidden_ref, bf16[1,512,3584]{2,1,0:T(8,128)(2,1)S(1)} %copy-done), custom_call_target="tpu_custom_call" | custom-call | flops 58720256 | tf_op jit(solution)/shard_map/leave/pallas_call | solution.py:156
  16.1 0.6 %collective-permute-done.1.arrived_ref = bf16[16,2,1792]{2,1,0:T(2,128)(2,1)S(1)} collective-permute-done((bf16[16,2,1792]{2,1,0:T(2,128)(2,1)S(1)}, bf16[16,2,1792]{2,1,0:T(2,128)(2,1)S(1)}, u32[]{:S(2)}, u32[]{:S(2)}) %collective-permute-start.1) | collective-permute-done | bytes 114720 | tf_op jit(solution)/shard_map/ppermute | solution.py:222
  16.7 0.1 add.1
  16.7 8.1 %all_to_all.11 = bf16[16,2,1792]{2,1,0:T(2,128)(2,1)S(1)} all-to-all(bf16[16,2,1792]{2,1,0:T(2,128)(2,1)S(1)} %add.1), channel_id=1, replica_groups={{11,10,1,0,3,2,5,4,7,6,9,8,13,12,15,14},{27,26,17,16,19,18,21,20,23,22,..., dimensions={0} | all-to-all | bytes 229376 | tf_op jit(solution)/shard_map/all_to_all | solution.py:194
  24.9 0.9 %combine.1 = bf16[32,3584]{1,0:T(8,128)(2,1)} custom-call(bf16[16,32]{1,0:T(8,128)(2,1)S(1)} %get-tuple-element.11.weight_ref, bf16[8,2,2,1792]{3,2,1,0:T(2,128)(2,1)S(1)} %bitcast.4), custom_call_target="tpu_custom_call" | custom-call | tf_op jit(solution)/shard_map/combine/pallas_call | solution.py:156
Async XLA Ops:
  0.0 13.1 %copy-start = (bf16[1,512,3584]{2,1,0:T(8,128)(2,1)S(1)}, bf16[1,512,3584]{2,1,0:T(8,128)(2,1)}, u32[]{:S(2)}) copy-start(bf16[1,512,3584]{2,1,0:T(8,128)(2,1)} %down_ref.5) | copy-start | bytes 11010052
  0.0 13.1 %copy-start.1 = (bf16[1,3584,512]{2,1,0:T(8,128)(2,1)S(1)}, bf16[1,3584,512]{2,1,0:T(8,128)(2,1)}, u32[]{:S(2)}) copy-start(bf16[1,3584,512]{2,1,0:T(8,128)(2,1)} %gate_ref.3) | copy-start | bytes 11010052
  0.0 13.1 %copy-start.2 = (bf16[1,3584,512]{2,1,0:T(8,128)(2,1)S(1)}, bf16[1,3584,512]{2,1,0:T(8,128)(2,1)}, u32[]{:S(2)}) copy-start(bf16[1,3584,512]{2,1,0:T(8,128)(2,1)} %up_ref.3) | copy-start | bytes 11010052
  12.8 1.3 %collective-permute-start = (bf16[16,2,1792]{2,1,0:T(2,128)(2,1)S(1)}, bf16[16,2,1792]{2,1,0:T(2,128)(2,1)S(1)}, u32[]{:S(2)}, u32[]{:S(2)}) collective-permute-start(bf16[16,2,1792]{2,1,0:T(2,128)(2,1)S(1)} %all_to_all.10.own_ref), channel_id=1, source_target_pairs={{0,1},{1,0},{2,3},{3,2},{4,5},{5,4},{6,7},{7,6},{8,9},{9,8},{10,11... | collective-permute-start | bytes 344072 | tf_op jit(solution)/shard_map/ppermute | solution.py:199
  15.3 1.4 %collective-permute-start.1 = (bf16[16,2,1792]{2,1,0:T(2,128)(2,1)S(1)}, bf16[16,2,1792]{2,1,0:T(2,128)(2,1)S(1)}, u32[]{:S(2)}, u32[]{:S(2)}) collective-permute-start(bf16[16,2,1792]{2,1,0:T(2,128)(2,1)S(1)} %get-tuple-element.16), channel_id=1, source_target_pairs={{0,1},{1,0},{2,3},{3,2},{4,5},{5,4},{6,7},{7,6},{8,9},{9,8},{10,11... | collective-permute-start | bytes 344072 | tf_op jit(solution)/shard_map/ppermute | solution.py:222
